TPU v7x, 32 devices: a whole 2x2x4 slice. The times are simulated.
32 devices in a mesh: lat: 4 (over y, x), lon: 8 (over z, core).
Axes of the slice: x: 2, y: 2, z: 4, core: 2. Of those that a mesh axis runs over, the one named last changes fastest.
Arguments:
- tokens: bfloat16 [32, 128, 1024], P('lat', 'lon'), may hold values from -60 to 60
- norm1_gain: float32 [1024], replicated, may hold values from 0.5 to 1.5
- conv_weight: float32 [3, 3, 1024], replicated, may hold values from -1.5 to 1.5
- norm2_gain: float32 [1024], replicated, may hold values from 0.5 to 1.5
- w_query: bfloat16 [1024, 1024], replicated, may hold values from -1 to 1
- w_key: bfloat16 [1024, 1024], replicated, may hold values from -1 to 1
- w_value: bfloat16 [1024, 1024], replicated, may hold values from -0.1875 to 0.1875
- w_out: bfloat16 [1024, 1024], replicated, may hold values from -0.1875 to 0.1875
- head_scale: float32 [16], replicated, may hold values from 4 to 32
- pattern: int32 [4, 8, 8], P('lat', 'lon'), may hold values from 0 to 31, as said below
Outputs:
- result: bfloat16 [32, 128, 1024], P('lat', 'lon')
Inputs may be any that keep to these rules, and one draw needn't show every extreme that they name: `pattern`: each row lists 8 different tiles; the first is the query tile itself; every listed tile lies in the query's band or a neighbouring band, in the query's longitude sector (the tiles of one device along `lon`) or one of the two sectors beside it around the globe; every query tile of the first and last band also lists both tiles of its own band two sectors away on either side around the globe; query tiles of other bands never list such tiles.
All inputs are finite; a program needn't handle non-finite values.
Results may differ from a plain program's by a relative error of at most 0.018.
Values may be sent and summed in bfloat16 or wider, within the bound.
No kernel may reach another device: no remote copies, remote signals or barrier semaphores. Data moves between devices by JAX's collectives and lax.ppermute only.
A program may use at most 64 MiB of HBM per device.

v0:
```python
import math

import jax
import jax.numpy as jnp
from jax import lax
from jax.sharding import PartitionSpec as P

TILE_LON = 16


def extended(cells, sides, width, closed):
    for axis, dim in sides:
        count = lax.axis_size(axis)
        ends = count if closed else count - 1
        head = lax.slice_in_dim(cells, 0, width, axis=dim)
        tail = lax.slice_in_dim(cells, cells.shape[dim] - width, cells.shape[dim], axis=dim)
        cells = jnp.concatenate(
            [
                lax.ppermute(tail, axis, [(i, (i + 1) % count) for i in range(ends)]),
                cells,
                lax.ppermute(head, axis, [((i + 1) % count, i) for i in range(ends)]),
            ],
            axis=dim,
        )
    return cells


def from_behind(value, axis, by):
    devices = lax.axis_size(axis)
    return lax.ppermute(value, axis, [(i, (i + by) % devices) for i in range(devices)])


def rms_norm(values, gain):
    widened = values.astype(jnp.float32)
    return widened * lax.rsqrt(jnp.mean(widened * widened, axis=-1, keepdims=True) + 1e-06) * gain


def head_norm(values):
    return values * lax.rsqrt(jnp.mean(values * values, axis=-1, keepdims=True) + 1e-06)


def on_device(
    tokens, norm1_gain, conv_weight, norm2_gain, w_query, w_key, w_value, w_out, head_scale, pattern
):
    lat_rows, lon_cols, model_width = tokens.shape
    tile_count = lon_cols // TILE_LON
    tile_size = lat_rows * TILE_LON
    head_count = head_scale.shape[0]
    head_size = model_width // head_count
    key_count = pattern.shape[2]
    normed = rms_norm(tokens, norm1_gain).astype(jnp.bfloat16)
    widened = extended(normed, (("lon", 1),), 1, True)
    conv_input = extended(widened, (("lat", 0),), 1, False)
    conv_sum = jnp.zeros(tokens.shape, jnp.float32)
    for row_off in range(3):
        for col_off in range(3):
            window = conv_input[row_off : row_off + lat_rows, col_off : col_off + lon_cols].astype(
                jnp.float32
            )
            conv_sum = conv_sum + window * conv_weight[row_off, col_off]
    hidden = (tokens.astype(jnp.float32) + conv_sum).astype(jnp.bfloat16)
    second = (
        rms_norm(hidden, norm2_gain).astype(jnp.bfloat16).reshape(lat_rows * lon_cols, model_width)
    )
    queries = head_norm(
        jnp.dot(second, w_query, preferred_element_type=jnp.float32).reshape(
            -1, head_count, head_size
        )
    )
    keys_own = head_norm(
        jnp.dot(second, w_key, preferred_element_type=jnp.float32).reshape(
            -1, head_count, head_size
        )
    )
    values_own = jnp.dot(second, w_value, preferred_element_type=jnp.float32).astype(jnp.bfloat16)
    queries = queries.astype(jnp.bfloat16).reshape(
        lat_rows, tile_count, TILE_LON, head_count, head_size
    )
    query_tiles = jnp.transpose(queries, (1, 0, 2, 3, 4)).reshape(
        tile_count, tile_size, head_count, head_size
    )
    key_value = jnp.concatenate(
        [keys_own.astype(jnp.bfloat16).reshape(-1, model_width), values_own], axis=-1
    )
    key_value = key_value.reshape(lat_rows, lon_cols, 2 * model_width)
    band_stack = extended(key_value, (("lat", 0),), lat_rows, False)
    kv_block = extended(band_stack, (("lon", 1),), lon_cols, True)
    east_block = from_behind(key_value, "lon", -2)
    west_block = from_behind(key_value, "lon", 2)
    near_tiles = kv_block.reshape(3, lat_rows, 3 * tile_count, TILE_LON, 2 * model_width)
    near_tiles = jnp.transpose(near_tiles, (0, 2, 1, 3, 4)).reshape(
        9 * tile_count, tile_size, 2 * model_width
    )

    def far_tiles(kv_far):
        shaped = kv_far.reshape(lat_rows, tile_count, TILE_LON, 2 * model_width)
        return jnp.transpose(shaped, (1, 0, 2, 3)).reshape(tile_count, tile_size, 2 * model_width)

    all_tiles = jnp.concatenate([near_tiles, far_tiles(west_block), far_tiles(east_block)], axis=0)
    sector_total = lax.axis_size("lon")
    tile_cols = tile_count * sector_total
    own_band = lax.axis_index("lat")
    own_sector = lax.axis_index("lon")
    tile_ids = pattern[0]
    key_band = tile_ids // tile_cols
    key_col = tile_ids % tile_cols
    key_sector = key_col // tile_count
    tile_pos = key_col % tile_count
    sector_off = (key_sector - own_sector) % sector_total
    sector_off = jnp.where(sector_off > sector_total // 2, sector_off - sector_total, sector_off)
    band_off = key_band - own_band
    near_slot = ((band_off + 1) * 3 + sector_off + 1) * tile_count + tile_pos
    slot_ids = jnp.where(
        jnp.abs(sector_off) <= 1,
        near_slot,
        jnp.where(sector_off < 0, 9 * tile_count + tile_pos, 10 * tile_count + tile_pos),
    )
    factor = head_scale * (1.0 / math.sqrt(head_size))

    def one_tile(item):
        own_queries, own_slots = item
        selected = jnp.take(all_tiles, own_slots, axis=0).reshape(
            key_count * tile_size, 2 * model_width
        )
        keys_sel = selected[:, :model_width].reshape(key_count * tile_size, head_count, head_size)
        values_sel = selected[:, model_width:].reshape(key_count * tile_size, head_count, head_size)
        scores = jnp.einsum(
            "qhe,khe->hqk", own_queries, keys_sel, preferred_element_type=jnp.float32
        )
        scores = scores * factor[:, None, None]
        row_max = jnp.max(scores, axis=-1, keepdims=True)
        exponent = jnp.exp(scores - row_max)
        attn_weights = (exponent / jnp.sum(exponent, axis=-1, keepdims=True)).astype(jnp.bfloat16)
        mixed = jnp.einsum(
            "hqk,khe->qhe", attn_weights, values_sel, preferred_element_type=jnp.float32
        )
        return mixed.astype(jnp.bfloat16)

    attended = lax.map(one_tile, (query_tiles, slot_ids))
    attended = attended.reshape(tile_count, lat_rows, TILE_LON, model_width)
    attended = jnp.transpose(attended, (1, 0, 2, 3)).reshape(lat_rows * lon_cols, model_width)
    projected = jnp.dot(attended, w_out, preferred_element_type=jnp.float32)
    result = hidden.astype(jnp.float32).reshape(lat_rows * lon_cols, model_width) + projected
    return result.astype(jnp.bfloat16).reshape(lat_rows, lon_cols, model_width)


def solution(mesh):
    return jax.shard_map(
        on_device,
        mesh=mesh,
        in_specs=(
            P("lat", "lon", None),
            P(),
            P(),
            P(),
            P(),
            P(),
            P(),
            P(),
            P(),
            P("lat", "lon", None),
        ),
        out_specs=P("lat", "lon", None),
        check_vma=False,
    )
```

profile of v0, /device:TPU:14, one launch (start us, length us, event | category | flops | bytes accessed | tf_op | source)
XLA Modules:
  0.0 145.7 jit_solution(6880251186730342307)
XLA Ops:
  0.0 1.2 fusion.10
  1.2 1.1 fusion.12
  2.3 0.1 fusion.22
  2.4 0.1 collective-permute-start
  2.5 0.0 copy-start.8
  2.5 1.7 %collective-permute-start.1 = (bf16[8,1,1024]{2,1,0:T(2,128)(2,1)S(1)}, bf16[8,1,1024]{2,1,0:T(2,128)(2,1)S(1)}, u32[]{:S(2)}, u32[]{:S(2)}) collective-permute-start(bf16[8,1,1024]{2,1,0:T(2,128)(2,1)S(1)} %get-tuple-element.32), channel_id=1, source_target_pairs={{1,0},{2,1},{3,2},{4,3},{5,4},{6,5},{7,6},{0,7},{9,8},{10,9},{11,1... | collective-permute-start | bytes 49160 | tf_op jit(solution)/shard_map/ppermute | solution.py:21
  4.2 1.6 %collective-permute-done = bf16[8,1,1024]{2,1,0:T(2,128)(2,1)S(1)} collective-permute-done((bf16[8,1,1024]{2,1,0:T(2,128)(2,1)S(1)}, bf16[8,1,1024]{2,1,0:T(2,128)(2,1)S(1)}, u32[]{:S(2)}, u32[]{:S(2)}) %collective-permute-start) | collective-permute-done | bytes 16416 | tf_op jit(solution)/shard_map/ppermute | solution.py:19
  5.8 0.1 collective-permute-done.1
  6.0 1.3 collective-permute-start.2
  7.3 4.5 %collective-permute-start.3 = (bf16[1,18,1024]{2,1,0:T(8,128)(2,1)S(1)}, bf16[1,18,1024]{2,1,0:T(8,128)(2,1)S(1)}, u32[]{:S(2)}, u32[]{:S(2)}) collective-permute-start(bf16[1,18,1024]{2,1,0:T(8,128)(2,1)S(1)} %get-tuple-element.30), channel_id=1, source_target_pairs={{8,0},{16,8},{24,16},{9,1},{17,9},{25,17},{10,2},{18,10},{26,18},{... | collective-permute-start | bytes 110600 | tf_op jit(solution)/shard_map/ppermute | solution.py:21
  11.8 0.9 fusion.23
  12.8 4.0 %copy.16 = bf16[1024,1024]{0,1:T(8,128)(2,1)} copy(bf16[1024,1024]{1,0:T(8,128)(2,1)} %param.15) | data formatting | bytes 4194304 | tf_op args[5]
  16.7 0.0 collective-permute-done.2
  16.7 0.0 collective-permute-done.3
  16.7 0.3 maximum_maximum_fusion
  17.0 0.8 multiply_reduce_fusion.3
  17.8 0.1 multiply_convert_fusion.2
  18.0 0.3 copy-done.1
  18.3 0.7 multiply_reduce_fusion.2
  19.1 0.1 multiply_convert_fusion.1
  19.1 1.2 copy.17
  20.3 1.4 concatenate.42
  21.8 0.4 convolution_convert_fusion
  22.2 0.0 copy-start.9
  22.2 0.0 copy-start.10
  22.3 3.4 %collective-permute-start.5 = (bf16[8,16,2048]{2,1,0:T(8,128)(2,1)S(1)}, bf16[8,16,2048]{2,1,0:T(8,128)(2,1)S(1)}, u32[]{:S(2)}, u32[]{:S(2)}) collective-permute-start(bf16[8,16,2048]{2,1,0:T(8,128)(2,1)S(1)} %pad_maximum_fusion.3), channel_id=1, source_target_pairs={{8,0},{16,8},{24,16},{9,1},{17,9},{25,17},{10,2},{18,10},{26,18},{... | collective-permute-start | bytes 1572872 | tf_op jit(solution)/shard_map/ppermute | solution.py:21
  25.7 1.3 collective-permute-start.4
  27.0 10.9 %collective-permute-done.5 = bf16[8,16,2048]{2,1,0:T(8,128)(2,1)S(1)} collective-permute-done((bf16[8,16,2048]{2,1,0:T(8,128)(2,1)S(1)}, bf16[8,16,2048]{2,1,0:T(8,128)(2,1)S(1)}, u32[]{:S(2)}, u32[]{:S(2)}) %collective-permute-start.5) | collective-permute-done | bytes 524320 | tf_op jit(solution)/shard_map/ppermute | solution.py:21
  37.9 12.2 %collective-permute-done.4 = bf16[8,16,2048]{2,1,0:T(8,128)(2,1)S(1)} collective-permute-done((bf16[8,16,2048]{2,1,0:T(8,128)(2,1)S(1)}, bf16[8,16,2048]{2,1,0:T(8,128)(2,1)S(1)}, u32[]{:S(2)}, u32[]{:S(2)}) %collective-permute-start.4) | collective-permute-done | bytes 524320 | tf_op jit(solution)/shard_map/ppermute | solution.py:19
  50.2 1.4 pad_maximum_fusion.2
  51.6 0.5 collective-permute-start.6
  52.1 3.9 %copy.20 = bf16[1024,1024]{0,1:T(8,128)(2,1)} copy(bf16[1024,1024]{1,0:T(8,128)(2,1)} %param.14) | data formatting | bytes 4194304 | tf_op args[4]
  56.1 0.1 broadcast_bitcast_fusion
  56.2 1.3 collective-permute-start.8
  57.5 1.8 %collective-permute-start.9 = (bf16[8,16,2048]{2,1,0:T(8,128)(2,1)}, bf16[8,16,2048]{2,1,0:T(8,128)(2,1)S(1)}, u32[]{:S(2)}, u32[]{:S(2)}) collective-permute-start(bf16[8,16,2048]{2,1,0:T(8,128)(2,1)} %copy-done.7), channel_id=1, source_target_pairs={{0,6},{1,7},{2,0},{3,1},{4,2},{5,3},{6,4},{7,5},{8,14},{9,15},{10,... | collective-permute-start | bytes 1572872 | tf_op jit(solution)/shard_map/ppermute | solution.py:30
  59.3 3.1 %multiply_reduce_fusion.1 = (f32[128,16]{0,1:T(8,128)S(1)}, f32[128,16,64]{0,2,1:T(8,128)}) fusion(bf16[128,1024,1]{1,0,2:T(8,128)(2,1)S(1)} %bitcast.90, bf16[16,64,1024]{2,1,0:T(8,128)(2,1)} %bitcast.83), kind=kOutput, calls=%fused_computation.26 | convolution fusion | flops 268695552 | bytes 2891776 | tf_op jit(solution)/shard_map/dot_general | solution.py:66
  62.4 41.1 %collective-permute-done.7 = bf16[24,16,2048]{2,1,0:T(8,128)(2,1)} collective-permute-done((bf16[24,16,2048]{2,1,0:T(8,128)(2,1)}, bf16[24,16,2048]{2,1,0:T(8,128)(2,1)}, u32[]{:S(2)}, u32[]{:S(2)}) %collective-permute-start.7) | collective-permute-done | bytes 1572896 | tf_op jit(solution)/shard_map/ppermute | solution.py:21
  103.6 2.6 %pad_maximum_fusion.1 = bf16[24,48,2048]{2,1,0:T(8,128)(2,1)S(1)} fusion(bf16[24,16,2048]{2,1,0:T(8,128)(2,1)} %collective-permute-done.7, bf16[8,16,2048]{2,1,0:T(8,128)(2,1)} %copy-done.4, bf16[8,16,1024]{2,1,0:T(8,128)(2,1)S(1)} %bitcast.87, bf16[8,16,1024]{2,1,0:T(8,128)(2,1)S(1)} %concatenate.42, bf16[8,16,2048]{2,1,0:T(8,128)(2,1)} %copy-done.5, ...), kind=kLoop, calls=%fused_computation.7 | loop fusion | flops 28311552 | bytes 9437184 | tf_op jit(solution)/shard_map/concatenate | solution.py:17
  106.1 0.4 copy.18
  106.5 4.7 %collective-permute-done.9 = bf16[8,16,2048]{2,1,0:T(8,128)(2,1)S(1)} collective-permute-done((bf16[8,16,2048]{2,1,0:T(8,128)(2,1)}, bf16[8,16,2048]{2,1,0:T(8,128)(2,1)S(1)}, u32[]{:S(2)}, u32[]{:S(2)}) %collective-permute-start.9) | collective-permute-done | bytes 524320 | tf_op jit(solution)/shard_map/ppermute | solution.py:30
  111.3 3.2 %pad_maximum_fusion = bf16[11,128,2048]{2,1,0:T(8,128)(2,1)} fusion(bf16[1,128,2048]{2,1,0:T(8,128)(2,1)S(1)} %bitcast.94, bf16[1,128,2048]{2,1,0:T(8,128)(2,1)S(1)} %bitcast.93, bf16[9,128,2048]{2,1,0:T(8,128)(2,1)S(1)} %bitcast.79), kind=kLoop, calls=%fused_computation.6 | loop fusion | flops 5767168 | bytes 11534336 | tf_op jit(solution)/shard_map/concatenate | solution.py:99
  114.4 5.4 %gather_fusion = bf16[8,128,2048]{2,1,0:T(8,128)(2,1)} fusion(bf16[11,128,2048]{2,1,0:T(8,128)(2,1)} %pad_maximum_fusion, s32[1024]{0:T(1024)S(1)} %pad_clamp_fusion), kind=kCustom, calls=%fused_computation | custom fusion | bytes 8388640 | tf_op jit(solution)/shard_map/while/body/eval_jaxpr/jit(_take)/gather | solution.py:122
  119.9 6.4 %copy.19 = bf16[1024,2048]{0,1:T(8,128)(2,1)} copy(bf16[1024,2048]{1,0:T(8,128)(2,1)} %bitcast.81) | data formatting | bytes 8388608 | tf_op jit(solution)/shard_map/while/body/eval_jaxpr/jit(_take)/gather | solution.py:122
  126.3 2.6 %broadcast_select_fusion = bf16[1024,2048]{0,1:T(8,128)(2,1)S(1)} fusion(bf16[1024,2048]{0,1:T(8,128)(2,1)} %copy.19, pred[1024]{0:T(1024)(128)(4,1)S(1)} %broadcast_bitcast_fusion), kind=kLoop, calls=%fused_computation.10 | loop fusion | flops 2097152 | bytes 8389632 | tf_op jit(solution)/shard_map/while/body/eval_jaxpr/jit(_take)/select_n | solution.py:122
  128.9 2.4 %fusion.21 = (bf16[1024,1024]{0,1:T(8,128)(2,1)}, bf16[1024,1024]{0,1:T(8,128)(2,1)}) fusion(bf16[1024,2048]{0,1:T(8,128)(2,1)S(1)} %broadcast_select_fusion), kind=kLoop, calls=%fused_computation.78 | loop fusion | bytes 8388608 | tf_op jit(solution)/shard_map/while/body/eval_jaxpr/slice | solution.py:125
  131.3 7.4 %fusion.24 = (f32[16,128]{1,0:T(8,128)S(1)}, f32[16,128,1024]{2,1,0:T(8,128)}) fusion(f32[16]{0:T(128)S(1)} %broadcast_multiply_fusion, bf16[1024,16,64]{0,2,1:T(8,128)(2,1)} %bitcast.84, f32[128,16,64]{0,2,1:T(8,128)S(1)} %copy-done.6, f32[128,16]{0,1:T(8,128)S(1)} %add_rsqrt_fusion), kind=kOutput, calls=%fused_computation.81 | convolution fusion | flops 274990080 | bytes 11026496 | tf_op jit(solution)/shard_map/while/body/eval_jaxpr/sub | solution.py:132
  138.7 5.8 %fusion.6 = bf16[16,64,128]{2,1,0:T(8,128)(2,1)S(1)} fusion(bf16[1024,16,64]{0,2,1:T(8,128)(2,1)} %bitcast.92, f32[16,128,1024]{2,1,0:T(8,128)} %get-tuple-element.47, f32[16,128]{1,0:T(8,128)S(1)} %get-tuple-element.46), kind=kOutput, calls=%fused_computation.13 | convolution fusion | flops 272760832 | bytes 10756096 | tf_op jit(solution)/shard_map/while/body/eval_jaxpr/hqk,khe->qhe/dot_general | solution.py:134
  144.5 1.2 fusion.7
  (31 shorter events, 0.2 us)
Async XLA Ops:
  0.0 21.8 %copy-start = (bf16[1024,1024]{1,0:T(8,128)(2,1)S(1)}, bf16[1024,1024]{1,0:T(8,128)(2,1)}, u32[]{:S(2)}) copy-start(bf16[1024,1024]{1,0:T(8,128)(2,1)} %param.16) | copy-start | bytes 6291460
  0.0 17.0 %copy-start.2 = (bf16[8,16,1024]{2,1,0:T(8,128)(2,1)S(1)}, bf16[8,16,1024]{2,1,0:T(8,128)(2,1)}, u32[]{:S(2)}) copy-start(bf16[8,16,1024]{2,1,0:T(8,128)(2,1)} %param.10) | copy-start | bytes 786436
  2.4 3.4 %collective-permute-start = (bf16[8,1,1024]{2,1,0:T(2,128)(2,1)S(1)}, bf16[8,1,1024]{2,1,0:T(2,128)(2,1)S(1)}, u32[]{:S(2)}, u32[]{:S(2)}) collective-permute-start(bf16[8,1,1024]{2,1,0:T(2,128)(2,1)S(1)} %get-tuple-element.31), channel_id=1, source_target_pairs={{0,1},{1,2},{2,3},{3,4},{4,5},{5,6},{6,7},{7,0},{8,9},{9,10},{10,1... | collective-permute-start | bytes 49160 | tf_op jit(solution)/shard_map/ppermute | solution.py:19
  2.5 15.4 %copy-start.8 = (f32[1024]{0:T(1024)S(1)}, f32[1024]{0:T(1024)}, u32[]{:S(2)}) copy-start(f32[1024]{0:T(1024)} %param.13) | copy-start | bytes 12292
  2.5 3.5 %collective-permute-start.1 = (bf16[8,1,1024]{2,1,0:T(2,128)(2,1)S(1)}, bf16[8,1,1024]{2,1,0:T(2,128)(2,1)S(1)}, u32[]{:S(2)}, u32[]{:S(2)}) collective-permute-start(bf16[8,1,1024]{2,1,0:T(2,128)(2,1)S(1)} %get-tuple-element.32), channel_id=1, source_target_pairs={{1,0},{2,1},{3,2},{4,3},{5,4},{6,5},{7,6},{0,7},{9,8},{10,9},{11,1... | collective-permute-start | bytes 49160 | tf_op jit(solution)/shard_map/ppermute | solution.py:21
  6.0 10.7 %collective-permute-start.2 = (bf16[1,18,1024]{2,1,0:T(8,128)(2,1)S(1)}, bf16[1,18,1024]{2,1,0:T(8,128)(2,1)S(1)}, u32[]{:S(2)}, u32[]{:S(2)}) collective-permute-start(bf16[1,18,1024]{2,1,0:T(8,128)(2,1)S(1)} %get-tuple-element.29), channel_id=1, source_target_pairs={{0,8},{8,16},{16,24},{1,9},{9,17},{17,25},{2,10},{10,18},{18,26},{... | collective-permute-start | bytes 110600 | tf_op jit(solution)/shard_map/ppermute | solution.py:19
  7.3 9.4 %collective-permute-start.3 = (bf16[1,18,1024]{2,1,0:T(8,128)(2,1)S(1)}, bf16[1,18,1024]{2,1,0:T(8,128)(2,1)S(1)}, u32[]{:S(2)}, u32[]{:S(2)}) collective-permute-start(bf16[1,18,1024]{2,1,0:T(8,128)(2,1)S(1)} %get-tuple-element.30), channel_id=1, source_target_pairs={{8,0},{16,8},{24,16},{9,1},{17,9},{25,17},{10,2},{18,10},{26,18},{... | collective-permute-start | bytes 110600 | tf_op jit(solution)/shard_map/ppermute | solution.py:21
  16.7 1.6 %copy-start.1 = (bf16[1024,1024]{0,1:T(8,128)(2,1)S(1)}, bf16[1024,1024]{0,1:T(8,128)(2,1)}, u32[]{:S(2)}) copy-start(bf16[1024,1024]{0,1:T(8,128)(2,1)} %copy.16) | copy-start | bytes 6291460
  22.2 33.8 %copy-start.9 = (s32[1,1,8]{2,1,0:T(1,128)S(1)}, s32[1,1,8]{2,1,0:T(1,128)}, u32[]{:S(2)}) copy-start(s32[1,1,8]{2,1,0:T(1,128)} %param.19) | copy-start | bytes 100
  22.2 33.9 %copy-start.10 = (f32[16]{0:T(128)S(1)}, f32[16]{0:T(128)}, u32[]{:S(2)}) copy-start(f32[16]{0:T(128)} %param.18) | copy-start | bytes 196
  22.3 15.6 %copy-start.7 = (bf16[8,16,2048]{2,1,0:T(8,128)(2,1)}, bf16[8,16,2048]{2,1,0:T(8,128)(2,1)S(1)}, u32[]{:S(2)}) copy-start(bf16[8,16,2048]{2,1,0:T(8,128)(2,1)S(1)} %pad_maximum_fusion.3) | copy-start | bytes 1572868
  22.3 15.6 %collective-permute-start.5 = (bf16[8,16,2048]{2,1,0:T(8,128)(2,1)S(1)}, bf16[8,16,2048]{2,1,0:T(8,128)(2,1)S(1)}, u32[]{:S(2)}, u32[]{:S(2)}) collective-permute-start(bf16[8,16,2048]{2,1,0:T(8,128)(2,1)S(1)} %pad_maximum_fusion.3), channel_id=1, source_target_pairs={{8,0},{16,8},{24,16},{9,1},{17,9},{25,17},{10,2},{18,10},{26,18},{... | collective-permute-start | bytes 1572872 | tf_op jit(solution)/shard_map/ppermute | solution.py:21
  25.7 24.5 %collective-permute-start.4 = (bf16[8,16,2048]{2,1,0:T(8,128)(2,1)S(1)}, bf16[8,16,2048]{2,1,0:T(8,128)(2,1)S(1)}, u32[]{:S(2)}, u32[]{:S(2)}) collective-permute-start(bf16[8,16,2048]{2,1,0:T(8,128)(2,1)S(1)} %pad_maximum_fusion.3), channel_id=1, source_target_pairs={{0,8},{8,16},{16,24},{1,9},{9,17},{17,25},{2,10},{10,18},{18,26},{... | collective-permute-start | bytes 1572872 | tf_op jit(solution)/shard_map/ppermute | solution.py:19
  37.9 12.2 %copy-start.4 = (bf16[8,16,2048]{2,1,0:T(8,128)(2,1)}, bf16[8,16,2048]{2,1,0:T(8,128)(2,1)S(1)}, u32[]{:S(2)}) copy-start(bf16[8,16,2048]{2,1,0:T(8,128)(2,1)S(1)} %collective-permute-done.5) | copy-start | bytes 1572868
  50.2 1.4 copy-start.5
  51.6 52.0 %collective-permute-start.7 = (bf16[24,16,2048]{2,1,0:T(8,128)(2,1)}, bf16[24,16,2048]{2,1,0:T(8,128)(2,1)}, u32[]{:S(2)}, u32[]{:S(2)}) collective-permute-start(bf16[24,16,2048]{2,1,0:T(8,128)(2,1)} %pad_maximum_fusion.2), channel_id=1, source_target_pairs={{1,0},{2,1},{3,2},{4,3},{5,4},{6,5},{7,6},{0,7},{9,8},{10,9},{11,1... | collective-permute-start | bytes 4718600 | tf_op jit(solution)/shard_map/ppermute | solution.py:21
  51.6 52.0 %collective-permute-start.6 = (bf16[24,16,2048]{2,1,0:T(8,128)(2,1)}, bf16[24,16,2048]{2,1,0:T(8,128)(2,1)}, u32[]{:S(2)}, u32[]{:S(2)}) collective-permute-start(bf16[24,16,2048]{2,1,0:T(8,128)(2,1)} %pad_maximum_fusion.2), channel_id=1, source_target_pairs={{0,1},{1,2},{2,3},{3,4},{4,5},{5,6},{6,7},{7,0},{8,9},{9,10},{10,1... | collective-permute-start | bytes 4718600 | tf_op jit(solution)/shard_map/ppermute | solution.py:19
  56.2 50.3 %collective-permute-start.8 = (bf16[8,16,2048]{2,1,0:T(8,128)(2,1)}, bf16[8,16,2048]{2,1,0:T(8,128)(2,1)S(1)}, u32[]{:S(2)}, u32[]{:S(2)}) collective-permute-start(bf16[8,16,2048]{2,1,0:T(8,128)(2,1)} %copy-done.7), channel_id=1, source_target_pairs={{0,2},{1,3},{2,4},{3,5},{4,6},{5,7},{6,0},{7,1},{8,10},{9,11},{10,... | collective-permute-start | bytes 1572872 | tf_op jit(solution)/shard_map/ppermute | solution.py:30
  57.5 53.8 %collective-permute-start.9 = (bf16[8,16,2048]{2,1,0:T(8,128)(2,1)}, bf16[8,16,2048]{2,1,0:T(8,128)(2,1)S(1)}, u32[]{:S(2)}, u32[]{:S(2)}) collective-permute-start(bf16[8,16,2048]{2,1,0:T(8,128)(2,1)} %copy-done.7), channel_id=1, source_target_pairs={{0,6},{1,7},{2,0},{3,1},{4,2},{5,3},{6,4},{7,5},{8,14},{9,15},{10,... | collective-permute-start | bytes 1572872 | tf_op jit(solution)/shard_map/ppermute | solution.py:30
  128.9 2.4 %copy-start.6 = (f32[128,16,64]{0,2,1:T(8,128)S(1)}, f32[128,16,64]{0,2,1:T(8,128)}, u32[]{:S(2)}) copy-start(f32[128,16,64]{0,2,1:T(8,128)} %get-tuple-element.45) | copy-start | bytes 1572868
  138.7 5.8 %copy-start.3 = (bf16[1024,1024]{1,0:T(8,128)(2,1)S(1)}, bf16[1024,1024]{1,0:T(8,128)(2,1)}, u32[]{:S(2)}) copy-start(bf16[1024,1024]{1,0:T(8,128)(2,1)} %param.17) | copy-start | bytes 6291460
where the time goes:
time: 146 us
  waiting for transfers between devices  70.8 us (48%)
  local copies, waits for them, and re-layouts  26.6 us (18%)
  matrix products  18.7 us (13%)
  starting transfers between devices  15.9 us (11%)
  other arithmetic  13.6 us (9%)
    ppermute x4, waiting for transfers between devices, extended(): lax.ppermute(head, axis, [((i + 1) % count, i) for i in range(ends)])  52.2 us
    ppermute x4, waiting for transfers between devices, extended(): lax.ppermute(tail, axis, [(i, (i + 1) % count) for i in range(ends)])  13.8 us
    gather x2, local copies, waits for them, and re-layouts, one_tile(): jnp.take(all_tiles, own_slots, axis=0)  11.8 us
    ppermute x4, starting transfers between devices, extended(): lax.ppermute(head, axis, [((i + 1) % count, i) for i in range(ends)])  9.64 us
    unnamed x24, local copies, waits for them, and re-layouts  8.27 us
    sub x1, matrix products, one_tile(): exponent = jnp.exp(scores - row_max)  7.41 us
    dot_general x1, matrix products, one_tile(): jnp.einsum('hqk,khe->qhe', attn_weights, values_sel, preferred_element_ty...  5.8 us
    ppermute x2, waiting for transfers between devices, from_behind(): lax.ppermute(value, axis, [(i, (i + by) % devices) for i in range(devices)])  4.74 us
  transfers between devices with their start and end apart: 10, of which 6 were waited for; matrix products, arithmetic and copies ran while one was open for 10% of the time, Pallas kernels for 0%

commit v1 on v0

v1 whole, which is shorter than its diff:
```python
import functools
import math

import jax
import jax.numpy as jnp
from jax import lax
from jax.experimental import pallas as pl
from jax.experimental.pallas import tpu as pltpu
from jax.sharding import PartitionSpec as P

EPS = 1e-06
HALO = 7
BIG = 1e30
VMEM = pl.BlockSpec(memory_space=pltpu.VMEM)
SMEM = pl.BlockSpec(memory_space=pltpu.SMEM)


def pair_swaps(count, first):
    pairs = []
    for low in range(first, count - 1, 2):
        pairs += [(low, low + 1), (low + 1, low)]
    return pairs


def lon_pairs(lats, lat_count, lon_count, off_chip):
    pairs = []
    for lat in lats:
        for low in range(1 if off_chip else 0, lon_count, 2):
            one, two = lat * lon_count + low, lat * lon_count + (low + 1) % lon_count
            pairs += [(one, two), (two, one)]
    return pairs


def two_away(count, first):
    pairs = []
    for start in range(first, count, 4):
        for low in (start, start + 1):
            if low + 2 < count:
                pairs += [(low, low + 2), (low + 2, low)]
    return pairs


def permuted(value, axis, pairs):
    if not pairs:
        return jnp.zeros_like(value)
    return lax.ppermute(value, axis, pairs)


def unit(values):
    return lax.rsqrt(jnp.mean(values * values, axis=-1, keepdims=True) + EPS)


def conv_kernel(
    meta, tok, tile_a, tile_b, halo, halo_a, halo_b, ring_a, ring_b, gain1, weight, gain2,
    hidden, second, second_a, second_b, window,
):
    rows, cols, width = tok.shape
    left, main = HALO, slice(HALO + 1, HALO + 1 + cols)
    right = HALO + 1 + cols
    gain_one, gain_two = gain1[...], gain2[...]

    def normed(raw):
        wide = raw.astype(jnp.float32)
        gain = gain_one if wide.ndim == 2 else gain_one[None]
        return (wide * unit(wide) * gain).astype(jnp.bfloat16).astype(jnp.float32)

    def place(base, raw, edges):
        for row in range(rows):
            window[base + row, main, :] = normed(raw[row])
        sides = normed(edges[...])
        for row in range(rows):
            window[base + row, left : left + 1, :] = sides[row : row + 1]
            window[base + row, right : right + 1, :] = sides[rows + row : rows + row + 1]

    def ring(row, data, bottom):
        base = pl.multiple_of(bottom * cols, cols)
        window[row, main, :] = normed(data[pl.ds(base, cols), :])
        sides = normed(data[2 * cols :, :])
        first, last = sides[0:1], sides[rows - 1 : rows]
        window[row, left : left + 1, :] = jnp.where(bottom > 0, last, first)
        first, last = sides[rows : rows + 1], sides[2 * rows - 1 : 2 * rows]
        window[row, right : right + 1, :] = jnp.where(bottom > 0, last, first)

    odd, high = meta[10], meta[11]
    base_own = 1 + rows
    base_a = jnp.where(odd > 0, 1, 1 + 2 * rows)
    base_b = jnp.where(odd > 0, 1 + 2 * rows, 1)
    last_row = 1 + 3 * rows
    place(base_own, tok, halo)
    place(base_a, tile_a, halo_a)
    place(base_b, tile_b, halo_b)
    ring(jnp.where(high > 0, 0, last_row), ring_a, high)
    ring(jnp.where(high > 0, last_row, 0), ring_b, 1 - high)

    for base, raw, out, keep in (
        (base_own, tok, second, True), (base_a, tile_a, second_a, False), (base_b, tile_b, second_b, False),
    ):
        def step(row, carry, base=base, raw=raw, out=out, keep=keep):
            total = None
            for down in range(3):
                for along in range(3):
                    part = window[base + row + down - 1, pl.ds(left + along, cols), :]
                    part = part * weight[3 * down + along : 3 * down + along + 1, :]
                    total = part if total is None else total + part
            mixed = (raw[row].astype(jnp.float32) + total).astype(jnp.bfloat16)
            wide = mixed.astype(jnp.float32)
            at = pl.ds(pl.multiple_of(row * cols, cols), cols)
            out[at, :] = (wide * unit(wide) * gain_two).astype(jnp.bfloat16)
            if keep:
                hidden[at, :] = mixed
            return carry

        lax.fori_loop(0, rows, step, 0)


def head_units(wide, spread):
    square = wide * wide
    high = square.astype(jnp.bfloat16)
    low = (square - high.astype(jnp.float32)).astype(jnp.bfloat16)
    mean = jnp.dot(high, spread, preferred_element_type=jnp.float32)
    mean += jnp.dot(low, spread, preferred_element_type=jnp.float32)
    return (wide * lax.rsqrt(mean + EPS)).astype(jnp.bfloat16)


def spread_matrix(size, head):
    row = lax.broadcasted_iota(jnp.int32, (size, size), 0) // head
    col = lax.broadcasted_iota(jnp.int32, (size, size), 1) // head
    return jnp.where(row == col, 1.0 / head, 0.0).astype(jnp.bfloat16)


CHUNK = 256


def keys_values(tokens, w_key, w_value, keys, values, head):
    spread = spread_matrix(CHUNK, head)
    for start in range(0, w_key.shape[1], CHUNK):
        part = slice(start, start + CHUNK)
        raw = jnp.dot(tokens, w_key[:, part], preferred_element_type=jnp.float32)
        keys[:, part] = head_units(raw, spread)
        raw = jnp.dot(tokens, w_value[:, part], preferred_element_type=jnp.float32)
        values[:, part] = raw.astype(jnp.bfloat16)


def attend(queries, keys, values, pair, width, head, slots, flags, scales):
    size = queries.shape[0]
    lanes = slice(pair * width, (pair + 1) * width)
    query = queries[:, lanes]
    lane = lax.broadcasted_iota(jnp.int32, query.shape, 1)
    zero = jnp.zeros_like(query)
    both = jnp.concatenate(
        [jnp.where(lane < head, query, zero), jnp.where(lane < head, zero, query)], axis=0
    )
    scores = lax.dot_general(
        both, keys[:, lanes], (((1,), (1,)), ((), ())), preferred_element_type=jnp.float32
    )
    top, low, mixed = [], [], []
    weights = []
    for half in range(2):
        part = scores[half * size : (half + 1) * size]
        scale = scales[2 * pair + half]
        best = None
        for slot in range(slots):
            at = part[:, slot * size : (slot + 1) * size]
            peak = jnp.max(at, axis=-1, keepdims=True) - flags[slot]
            best = peak if best is None else jnp.maximum(best, peak)
        rows = []
        for slot in range(slots):
            at = part[:, slot * size : (slot + 1) * size]
            rows.append(jnp.exp2((at - (best + flags[slot])) * scale))
        exps = jnp.concatenate(rows, axis=1)
        low.append(jnp.sum(exps, axis=-1, keepdims=True))
        top.append(best * scale)
        weights.append(exps.astype(jnp.bfloat16))
    mixed = jnp.dot(
        jnp.concatenate(weights, axis=0), values[:, lanes], preferred_element_type=jnp.float32
    )
    lane = lax.broadcasted_iota(jnp.int32, (size, width), 1)
    return top, low, jnp.where(lane < head, mixed[:size], mixed[size:])


def columns(parts, size):
    lane = lax.broadcasted_iota(jnp.int32, (size, 128), 1)
    out = jnp.zeros((size, 128), jnp.float32)
    for index, part in enumerate(parts):
        out = jnp.where(lane == index, part, out)
    return out


def near_kernel(
    heads, meta, scale_in, own, own_a, own_b, on, on_a, on_b, w_query, w_key, w_value,
    query_out, top_out, low_out, mixed_out, keys, values,
):
    size, model = own.shape
    head = model // heads
    spread = spread_matrix(CHUNK, head)
    first = own[...]
    for start in range(0, model, CHUNK):
        part = slice(start, start + CHUNK)
        raw = jnp.dot(first, w_query[:, part], preferred_element_type=jnp.float32)
        query_out[:, part] = head_units(raw, spread)
    tokens = jnp.concatenate([ref[...] for ref in (own, own_a, own_b, on, on_a, on_b)], axis=0)
    keys_values(tokens, w_key, w_value, keys, values, head)
    flags = [jnp.where(meta[slot] > 0, 0.0, BIG).astype(jnp.float32) for slot in range(6)]
    factor = math.log2(math.e) / math.sqrt(head)
    scales = [scale_in[index] * factor for index in range(heads)]
    tops, lows = [], []
    for pair in range(heads // 2):
        top, low, mixed = attend(
            query_out, keys, values, pair, 2 * head, head, 6, flags, scales
        )
        tops += top
        lows += low
        mixed_out[:, 2 * head * pair : 2 * head * (pair + 1)] = mixed
    top_out[...] = columns(tops, size)
    low_out[...] = columns(lows, size)


def far_kernel(
    heads, meta, scale_in, off, off_a, off_b, off_x, on_y, w_key, w_value, w_out,
    queries, tops, lows, mixeds, hidden, result, keys, values, joined,
):
    size, model = off.shape
    head = model // heads
    polar = meta[12] > 0
    third = jnp.where(polar, off_x[...], off_b[...])
    tokens = jnp.concatenate([off[...], off_a[...], third, on_y[...]], axis=0)
    keys_values(tokens, w_key, w_value, keys, values, head)
    flags = [jnp.where(meta[6 + slot] > 0, 0.0, BIG).astype(jnp.float32) for slot in range(4)]
    factor = math.log2(math.e) / math.sqrt(head)
    scales = [scale_in[index] * factor for index in range(heads)]
    old_top, old_low = tops[...], lows[...]
    lane = lax.broadcasted_iota(jnp.int32, (size, 2 * head), 1)
    for pair in range(heads // 2):
        top, low, mixed = attend(queries, keys, values, pair, 2 * head, head, 4, flags, scales)
        before, after = [], []
        for half in range(2):
            index = 2 * pair + half
            was = old_top[:, index : index + 1]
            best = jnp.maximum(was, top[half])
            old, new = jnp.exp2(was - best), jnp.exp2(top[half] - best)
            share = 1.0 / (old * old_low[:, index : index + 1] + new * low[half])
            before.append(old * share)
            after.append(new * share)
        at = slice(2 * head * pair, 2 * head * (pair + 1))
        kept = mixeds[:, at] * jnp.where(lane < head, before[0], before[1])
        added = mixed * jnp.where(lane < head, after[0], after[1])
        joined[:, at] = (kept + added).astype(jnp.bfloat16)
    attended = joined[...]
    for start in range(0, model, CHUNK):
        part = slice(start, start + CHUNK)
        out = jnp.dot(attended, w_out[:, part], preferred_element_type=jnp.float32)
        result[:, part] = (hidden[:, part].astype(jnp.float32) + out).astype(jnp.bfloat16)


def on_device(
    tokens, norm1_gain, conv_weight, norm2_gain, w_query, w_key, w_value, w_out, head_scale, pattern
):
    rows, cols, model = tokens.shape
    size = rows * cols
    heads = head_scale.shape[0]
    lats, lons = lax.axis_size("lat"), lax.axis_size("lon")
    band, sector = lax.axis_index("lat"), lax.axis_index("lon")
    every = range(lats)
    inner = range(1, lats - 1)
    poles = (0, lats - 1)
    both = ("lat", "lon")

    swap_a = functools.partial(permuted, axis="lat", pairs=pair_swaps(lats, 0))
    swap_b = functools.partial(permuted, axis="lat", pairs=pair_swaps(lats, 1))

    def across(value, off_chip, bands=every):
        return permuted(value, both, lon_pairs(bands, lats, lons, off_chip))

    even_band = band % 2 == 0
    band_a = jnp.where(even_band, band + 1, band - 1)
    band_b = jnp.where(even_band, band - 1, band + 1)
    polar = (band == 0) | (band == lats - 1)
    even_sector = sector % 2 == 0

    def on_of(place):
        return jnp.where(place % 2 == 0, place + 1, place - 1)

    def off_of(place):
        return jnp.where(place % 2 == 0, place - 1 + lons, place + 1) % lons

    on_sector, off_sector = on_of(sector), off_of(sector)
    places = [
        (band, sector), (band_a, sector), (band_b, sector),
        (band, on_sector), (band_a, on_sector), (band_b, on_sector),
        (band, off_sector), (band_a, off_sector),
        (jnp.where(polar, band, band_b), jnp.where(polar, on_of(off_sector), off_sector)),
        (band, off_of(on_sector)),
    ]
    ids = jnp.stack([at_band * lons + at_sector for at_band, at_sector in places])
    exists = [True, True, ~polar, True, True, ~polar, True, True, True, polar]
    exists = jnp.stack([jnp.asarray(flag) for flag in exists])
    listed = jnp.any(pattern.reshape(-1)[None, :] == ids[:, None], axis=1) & exists
    extra = jnp.stack([~even_band, band % 4 >= 2, polar])
    meta = jnp.concatenate([listed, extra]).astype(jnp.int32)

    tile_a, tile_b = swap_a(tokens), swap_b(tokens)
    edges = jnp.concatenate([tokens[:, 0], tokens[:, cols - 1]], axis=0)
    on_edges, off_edges = across(edges, False), across(edges, True)
    halo = jnp.concatenate(
        [
            jnp.where(even_sector, off_edges[rows:], on_edges[rows:]),
            jnp.where(even_sector, on_edges[:rows], off_edges[:rows]),
        ],
        axis=0,
    )
    halo_a, halo_b = swap_a(halo), swap_b(halo)
    brink = jnp.concatenate([tokens[0], tokens[rows - 1], halo], axis=0)
    ring_a = permuted(brink, "lat", two_away(lats, 0))
    ring_b = permuted(brink, "lat", two_away(lats, 2))

    tile = jax.ShapeDtypeStruct((size, model), jnp.bfloat16)
    limit = pltpu.CompilerParams(vmem_limit_bytes=40 * 2**20)
    hidden, second, second_a, second_b = pl.pallas_call(
        conv_kernel,
        out_shape=[tile] * 4,
        in_specs=[SMEM] + [VMEM] * 11,
        out_specs=[VMEM] * 4,
        scratch_shapes=[pltpu.VMEM((2 + 3 * rows, 32, model), jnp.float32)],
        compiler_params=limit,
        name="conv",
    )(
        meta, tokens, tile_a, tile_b, halo, halo_a, halo_b, ring_a, ring_b,
        norm1_gain.reshape(1, model), conv_weight.reshape(9, model), norm2_gain.reshape(1, model),
    )

    on, on_a, on_b = across(second, False), across(second_a, False), across(second_b, False)
    off = across(second, True)
    off_a = across(second_a, True)
    off_b = across(second_b, True, inner)
    off_x = across(on, True, poles)
    on_y = across(off, False, poles)

    stats = jax.ShapeDtypeStruct((size, 128), jnp.float32)
    queries, tops, lows, mixed = pl.pallas_call(
        functools.partial(near_kernel, heads),
        out_shape=[tile, stats, stats, jax.ShapeDtypeStruct((size, model), jnp.float32)],
        in_specs=[SMEM, SMEM] + [VMEM] * 9,
        out_specs=[VMEM] * 4,
        scratch_shapes=[pltpu.VMEM((6 * size, model), jnp.bfloat16)] * 2,
        compiler_params=limit,
        cost_estimate=pl.CostEstimate(
            flops=2 * size * model * model * 13, bytes_accessed=8 * 2**20, transcendentals=0
        ),
        name="near",
    )(meta, head_scale, second, second_a, second_b, on, on_a, on_b, w_query, w_key, w_value)

    result = pl.pallas_call(
        functools.partial(far_kernel, heads),
        out_shape=tile,
        in_specs=[SMEM, SMEM] + [VMEM] * 13,
        out_specs=VMEM,
        scratch_shapes=[pltpu.VMEM((4 * size, model), jnp.bfloat16)] * 2
        + [pltpu.VMEM((size, model), jnp.bfloat16)],
        compiler_params=limit,
        cost_estimate=pl.CostEstimate(
            flops=2 * size * model * model * 9, bytes_accessed=8 * 2**20, transcendentals=0
        ),
        name="far",
    )(
        meta, head_scale, off, off_a, off_b, off_x, on_y, w_key, w_value, w_out,
        queries, tops, lows, mixed, hidden,
    )
    return result.reshape(rows, cols, model)


def solution(mesh):
    return jax.shard_map(
        on_device,
        mesh=mesh,
        in_specs=(
            P("lat", "lon", None),
            P(),
            P(),
            P(),
            P(),
            P(),
            P(),
            P(),
            P(),
            P("lat", "lon", None),
        ),
        out_specs=P("lat", "lon", None),
        check_vma=False,
    )
```

time: 146 us -> 67.1 us (0.46)
  the two profiles are of different devices: /device:TPU:14 before, /device:TPU:2 now
where the time goes in v1:
time: 67.1 us; the launch traced here: 65.8 us
  Pallas kernels  25 us (37%)
  starting transfers between devices  18.4 us (27%)
  waiting for transfers between devices  12.2 us (18%)
  local copies, waits for them, and re-layouts  9.17 us (14%)
  other arithmetic  0.86 us (1%)
    ppermute x15, starting transfers between devices, permuted(): return lax.ppermute(value, axis, pairs)  18.4 us
    ppermute x15, waiting for transfers between devices, permuted(): return lax.ppermute(value, axis, pairs)  12.2 us
    pallas_call x1, Pallas kernels, on_device(): pl.pallas_call(functools.partial(near_kernel, heads), out_shape=[tile, st...  10.5 us
    pallas_call x1, Pallas kernels, on_device(): pl.pallas_call(functools.partial(far_kernel, heads), out_shape=tile, in_s...  8.72 us
    unnamed x18, local copies, waits for them, and re-layouts  6.16 us
    pallas_call x1, Pallas kernels, on_device(): pl.pallas_call(conv_kernel, out_shape=[tile] * 4, in_specs=[SMEM] + [VMEM...  5.85 us
  transfers between devices with their start and end apart: 15, of which 4 were waited for; matrix products, arithmetic and copies ran while one was open for 4% of the time, Pallas kernels for 16%

profile of v1, /device:TPU:2, one launch (start us, length us, event | category | flops | bytes accessed | tf_op | source)
XLA Modules:
  0.0 65.8 jit_solution(9106278438511225709)
XLA Ops:
  0.0 1.2 %fusion = (bf16[8,1,1024]{2,1,0:T(2,128)(2,1)S(1)}, bf16[8,1,1024]{2,1,0:T(2,128)(2,1)S(1)}) fusion(bf16[8,16,1024]{2,1,0:T(8,128)(2,1)} %tok.1), kind=kLoop, calls=%fused_computation.11 | loop fusion | bytes 65536 | tf_op jit(solution)/shard_map/slice | solution.py:302
  1.2 3.1 %collective-permute-start.2 = (bf16[16,1024]{1,0:T(8,128)(2,1)S(1)}, bf16[16,1024]{1,0:T(8,128)(2,1)S(1)}, u32[]{:S(2)}, u32[]{:S(2)}) collective-permute-start(bf16[16,1024]{1,0:T(8,128)(2,1)S(1)} %pad_maximum_fusion.1), channel_id=1, source_target_pairs={{1,2},{2,1},{3,4},{4,3},{5,6},{6,5},{7,0},{0,7},{9,10},{10,9},{11,... | collective-permute-start | bytes 98312 | tf_op jit(solution)/shard_map/ppermute | solution.py:46
  4.3 0.0 collective-permute-start.3
  4.3 0.5 collective-permute-start
  4.9 4.3 %collective-permute-start.1 = (bf16[8,16,1024]{2,1,0:T(8,128)(2,1)}, bf16[8,16,1024]{2,1,0:T(8,128)(2,1)S(1)}, u32[]{:S(2)}, u32[]{:S(2)}) collective-permute-start(bf16[8,16,1024]{2,1,0:T(8,128)(2,1)} %tok.1), channel_id=1, source_target_pairs={{8,16},{16,8},{9,17},{17,9},{10,18},{18,10},{11,19},{19,11},{12,20... | collective-permute-start | bytes 786440 | tf_op jit(solution)/shard_map/ppermute | solution.py:46
  9.2 0.8 %slice_bitcast_fusion.1 = (bf16[16,1024]{1,0:T(8,128)(2,1)S(1)}, bf16[16,1024]{1,0:T(8,128)(2,1)S(1)}) fusion(bf16[8,16,1024]{2,1,0:T(8,128)(2,1)} %tok.1), kind=kLoop, calls=%fused_computation.4 | loop fusion | bytes 131072 | tf_op jit(solution)/shard_map/squeeze | solution.py:312
  10.0 0.1 stack.60
  10.1 0.7 %compare_reduce_fusion = pred[10]{0:T(512)(128)(4,1)S(1)} fusion(s32[10]{0:T(128)S(1)} %stack.60, s32[8]{0:T(128)} %bitcast.28), kind=kLoop, calls=%fused_computation.9 | loop fusion | flops 150 | bytes 82 | tf_op jit(solution)/shard_map/reduce_or | solution.py:297
  10.9 0.1 stack.63
  11.0 0.0 collective-permute-done.2
  11.0 0.0 collective-permute-done.3
  11.0 0.1 collective-permute-start.4
  11.1 2.4 %collective-permute-start.5 = (bf16[16,1024]{1,0:T(8,128)(2,1)S(1)}, bf16[16,1024]{1,0:T(8,128)(2,1)S(1)}, u32[]{:S(2)}, u32[]{:S(2)}) collective-permute-start(bf16[16,1024]{1,0:T(8,128)(2,1)S(1)} %pad_maximum_fusion.2.halo), channel_id=1, source_target_pairs={{8,16},{16,8},{9,17},{17,9},{10,18},{18,10},{11,19},{19,11},{12,20... | collective-permute-start | bytes 98312 | tf_op jit(solution)/shard_map/ppermute | solution.py:46
  13.5 0.1 collective-permute-start.6
  13.6 0.1 add_convert_fusion.meta
  13.7 0.8 %reshape.15.weight = f32[9,1024]{1,0:T(8,128)S(1)} reshape(f32[3,3,1024]{2,1,0:T(4,128)} %param.12) | data formatting | bytes 73728 | tf_op jit(solution)/shard_map/reshape | solution.py:328
  14.5 3.5 %collective-permute-done.4.halo_a = bf16[16,1024]{1,0:T(8,128)(2,1)S(1)} collective-permute-done((bf16[16,1024]{1,0:T(8,128)(2,1)S(1)}, bf16[16,1024]{1,0:T(8,128)(2,1)S(1)}, u32[]{:S(2)}, u32[]{:S(2)}) %collective-permute-start.4) | collective-permute-done | bytes 32800 | tf_op jit(solution)/shard_map/ppermute | solution.py:46
  18.0 3.3 %collective-permute-done.5.halo_b = bf16[16,1024]{1,0:T(8,128)(2,1)S(1)} collective-permute-done((bf16[16,1024]{1,0:T(8,128)(2,1)S(1)}, bf16[16,1024]{1,0:T(8,128)(2,1)S(1)}, u32[]{:S(2)}, u32[]{:S(2)}) %collective-permute-start.5) | collective-permute-done | bytes 32800 | tf_op jit(solution)/shard_map/ppermute | solution.py:46
  21.3 1.3 %collective-permute-done.6.ring_a = bf16[48,1024]{1,0:T(8,128)(2,1)S(1)} collective-permute-done((bf16[48,1024]{1,0:T(8,128)(2,1)S(1)}, bf16[48,1024]{1,0:T(8,128)(2,1)S(1)}, u32[]{:S(2)}, u32[]{:S(2)}) %collective-permute-start.6) | collective-permute-done | bytes 98336 | tf_op jit(solution)/shard_map/ppermute | solution.py:46
  22.6 0.0 collective-permute-done.tile_a
  22.6 0.0 collective-permute-done.1.tile_b
  22.7 0.0 copy-start.4
  22.7 0.9 %copy-done.4 = bf16[8,16,1024]{2,1,0:T(8,128)(2,1)S(1)} copy-done((bf16[8,16,1024]{2,1,0:T(8,128)(2,1)S(1)}, bf16[8,16,1024]{2,1,0:T(8,128)(2,1)}, u32[]{:S(2)}) %copy-start.4) | copy-done | bytes 262168
  23.6 0.7 %copy-done.5 = f32[1024]{0:T(1024)S(1)} copy-done((f32[1024]{0:T(1024)S(1)}, f32[1024]{0:T(1024)}, u32[]{:S(2)}) %copy-start.5) | copy-done | bytes 4120
  24.3 0.7 %copy-done.6 = f32[1024]{0:T(1024)S(1)} copy-done((f32[1024]{0:T(1024)S(1)}, f32[1024]{0:T(1024)}, u32[]{:S(2)}) %copy-start.6) | copy-done | bytes 4120
  25.0 5.8 %conv.1 = (bf16[128,1024]{1,0:T(8,128)(2,1)S(1)}, bf16[128,1024]{1,0:T(8,128)(2,1)S(1)}, bf16[128,1024]{1,0:T(8,128)(2,1)S(1)}, bf16[128,1024]{1,0:T(8,128)(2,1)S(1)}) custom-call(s32[13]{0:T(128)S(1)} %add_convert_fusion.meta, bf16[8,16,1024]{2,1,0:T(8,128)(2,1)S(1)} %copy-done.4, bf16[8,16,1024]{2,1,0:T(8,128)(2,1)S(1)} %collective-permute-done.tile_a, ...), custom_call_target="tpu_custom_call" | custom-call | tf_op jit(solution)/shard_map/conv/pallas_call | solution.py:318
  30.8 0.1 collective-permute-start.10
  30.9 0.5 collective-permute-start.13
  31.4 0.3 collective-permute-start.7
  31.7 0.0 collective-permute-start.14
  31.7 3.2 %collective-permute-start.8 = (bf16[128,1024]{1,0:T(8,128)(2,1)S(1)}, bf16[128,1024]{1,0:T(8,128)(2,1)S(1)}, u32[]{:S(2)}, u32[]{:S(2)}) collective-permute-start(bf16[128,1024]{1,0:T(8,128)(2,1)S(1)} %get-tuple-element.14.own_a), channel_id=1, source_target_pairs={{1,2},{2,1},{3,4},{4,3},{5,6},{6,5},{7,0},{0,7},{9,10},{10,9},{11,... | collective-permute-start | bytes 786440 | tf_op jit(solution)/shard_map/ppermute | solution.py:46
  35.0 0.0 collective-permute-done.10.on
  35.0 2.2 %collective-permute-start.9 = (bf16[128,1024]{1,0:T(8,128)(2,1)S(1)}, bf16[128,1024]{1,0:T(8,128)(2,1)S(1)}, u32[]{:S(2)}, u32[]{:S(2)}) collective-permute-start(bf16[128,1024]{1,0:T(8,128)(2,1)S(1)} %get-tuple-element.15.own_b), channel_id=1, source_target_pairs={{9,10},{10,9},{11,12},{12,11},{13,14},{14,13},{15,8},{8,15},{17,18... | collective-permute-start | bytes 786440 | tf_op jit(solution)/shard_map/ppermute | solution.py:46
  37.2 0.0 collective-permute-done.13.on_a
  37.2 0.7 %collective-permute-start.11 = (bf16[128,1024]{1,0:T(8,128)(2,1)S(1)}, bf16[128,1024]{1,0:T(8,128)(2,1)S(1)}, u32[]{:S(2)}, u32[]{:S(2)}) collective-permute-start(bf16[128,1024]{1,0:T(8,128)(2,1)S(1)} %collective-permute-done.10.on), channel_id=1, source_target_pairs={{1,2},{2,1},{3,4},{4,3},{5,6},{6,5},{7,0},{0,7},{25,26},{26,25},{2... | collective-permute-start | bytes 786440 | tf_op jit(solution)/shard_map/ppermute | solution.py:46
  37.9 4.0 %collective-permute-done.7.off = bf16[128,1024]{1,0:T(8,128)(2,1)S(1)} collective-permute-done((bf16[128,1024]{1,0:T(8,128)(2,1)S(1)}, bf16[128,1024]{1,0:T(8,128)(2,1)S(1)}, u32[]{:S(2)}, u32[]{:S(2)}) %collective-permute-start.7) | collective-permute-done | bytes 262176 | tf_op jit(solution)/shard_map/ppermute | solution.py:46
  41.9 0.8 %collective-permute-start.12 = (bf16[128,1024]{1,0:T(8,128)(2,1)S(1)}, bf16[128,1024]{1,0:T(8,128)(2,1)S(1)}, u32[]{:S(2)}, u32[]{:S(2)}) collective-permute-start(bf16[128,1024]{1,0:T(8,128)(2,1)S(1)} %collective-permute-done.7.off), channel_id=1, source_target_pairs={{0,1},{1,0},{2,3},{3,2},{4,5},{5,4},{6,7},{7,6},{24,25},{25,24},{2... | collective-permute-start | bytes 786440 | tf_op jit(solution)/shard_map/ppermute | solution.py:46
  42.7 0.0 collective-permute-done.14.on_b
  42.7 0.0 copy-start.1
  42.8 1.6 %copy-done.1 = bf16[1024,1024]{1,0:T(8,128)(2,1)S(1)} copy-done((bf16[1024,1024]{1,0:T(8,128)(2,1)S(1)}, bf16[1024,1024]{1,0:T(8,128)(2,1)}, u32[]{:S(2)}) %copy-start.1) | copy-done | bytes 2097176
  44.3 0.7 copy-done.7
  45.0 1.6 %copy-done.8 = bf16[1024,1024]{1,0:T(8,128)(2,1)S(1)} copy-done((bf16[1024,1024]{1,0:T(8,128)(2,1)S(1)}, bf16[1024,1024]{1,0:T(8,128)(2,1)}, u32[]{:S(2)}) %copy-start.8) | copy-done | bytes 2097176
  46.6 10.5 %near.1 = (bf16[128,1024]{1,0:T(8,128)(2,1)S(1)}, f32[128,128]{1,0:T(8,128)S(1)}, f32[128,128]{1,0:T(8,128)S(1)}, f32[128,1024]{1,0:T(8,128)S(1)}) custom-call(s32[13]{0:T(128)S(1)} %add_convert_fusion.meta, f32[16]{0:T(128)S(1)} %copy-done.7, bf16[128,1024]{1,0:T(8,128)(2,1)S(1)} %get-tuple-element.13.own, bf16[128,1024]{1,0:T(8,128)(2,1)S(1)} %get-tuple-element.14.own_a, ...), custom_call_target="tpu_custom_call" | custom-call | flops 3489660928 | bytes 8388608 | tf_op jit(solution)/shard_map/near/pallas_call | solution.py:339
  57.1 0.0 collective-permute-done.8.off_a
  57.1 0.0 collective-permute-done.9.off_b
  57.1 0.0 collective-permute-done.11.off_x
  57.1 0.0 collective-permute-done.12.on_y
  57.1 8.7 %far.1 = bf16[128,1024]{1,0:T(8,128)(2,1)} custom-call(s32[13]{0:T(128)S(1)} %add_convert_fusion.meta, f32[16]{0:T(128)S(1)} %copy-done.7, bf16[128,1024]{1,0:T(8,128)(2,1)S(1)} %collective-permute-done.7.off, bf16[128,1024]{1,0:T(8,128)(2,1)S(1)} %collective-permute-done.8.off_a, bf16[128,1024]{1,0:T(8,128)(2,1)S(1)} %collective-permute-done.9.off_b, ...), custom_call_target="tpu_custom_call" | custom-call | flops 2415919104 | bytes 8388608 | tf_op jit(solution)/shard_map/far/pallas_call | solution.py:352
  (18 shorter events, 0.1 us)
Async XLA Ops:
  0.0 42.7 %copy-start = (bf16[1024,1024]{1,0:T(8,128)(2,1)S(1)}, bf16[1024,1024]{1,0:T(8,128)(2,1)}, u32[]{:S(2)}) copy-start(bf16[1024,1024]{1,0:T(8,128)(2,1)} %w_key.3) | copy-start | bytes 6291460
  1.2 9.8 %collective-permute-start.2 = (bf16[16,1024]{1,0:T(8,128)(2,1)S(1)}, bf16[16,1024]{1,0:T(8,128)(2,1)S(1)}, u32[]{:S(2)}, u32[]{:S(2)}) collective-permute-start(bf16[16,1024]{1,0:T(8,128)(2,1)S(1)} %pad_maximum_fusion.1), channel_id=1, source_target_pairs={{1,2},{2,1},{3,4},{4,3},{5,6},{6,5},{7,0},{0,7},{9,10},{10,9},{11,... | collective-permute-start | bytes 98312 | tf_op jit(solution)/shard_map/ppermute | solution.py:46
  4.3 6.7 %collective-permute-start.3 = (bf16[16,1024]{1,0:T(8,128)(2,1)S(1)}, bf16[16,1024]{1,0:T(8,128)(2,1)S(1)}, u32[]{:S(2)}, u32[]{:S(2)}) collective-permute-start(bf16[16,1024]{1,0:T(8,128)(2,1)S(1)} %pad_maximum_fusion.1), channel_id=1, source_target_pairs={{0,1},{1,0},{2,3},{3,2},{4,5},{5,4},{6,7},{7,6},{8,9},{9,8},{10,11... | collective-permute-start | bytes 98312 | tf_op jit(solution)/shard_map/ppermute | solution.py:46
  4.3 18.3 %collective-permute-start = (bf16[8,16,1024]{2,1,0:T(8,128)(2,1)}, bf16[8,16,1024]{2,1,0:T(8,128)(2,1)S(1)}, u32[]{:S(2)}, u32[]{:S(2)}) collective-permute-start(bf16[8,16,1024]{2,1,0:T(8,128)(2,1)} %tok.1), channel_id=1, source_target_pairs={{0,8},{8,0},{16,24},{24,16},{1,9},{9,1},{17,25},{25,17},{2,10},{10... | collective-permute-start | bytes 786440 | tf_op jit(solution)/shard_map/ppermute | solution.py:46
  4.9 17.8 %collective-permute-start.1 = (bf16[8,16,1024]{2,1,0:T(8,128)(2,1)}, bf16[8,16,1024]{2,1,0:T(8,128)(2,1)S(1)}, u32[]{:S(2)}, u32[]{:S(2)}) collective-permute-start(bf16[8,16,1024]{2,1,0:T(8,128)(2,1)} %tok.1), channel_id=1, source_target_pairs={{8,16},{16,8},{9,17},{17,9},{10,18},{18,10},{11,19},{19,11},{12,20... | collective-permute-start | bytes 786440 | tf_op jit(solution)/shard_map/ppermute | solution.py:46
  11.0 7.0 %collective-permute-start.4 = (bf16[16,1024]{1,0:T(8,128)(2,1)S(1)}, bf16[16,1024]{1,0:T(8,128)(2,1)S(1)}, u32[]{:S(2)}, u32[]{:S(2)}) collective-permute-start(bf16[16,1024]{1,0:T(8,128)(2,1)S(1)} %pad_maximum_fusion.2.halo), channel_id=1, source_target_pairs={{0,8},{8,0},{16,24},{24,16},{1,9},{9,1},{17,25},{25,17},{2,10},{10... | collective-permute-start | bytes 98312 | tf_op jit(solution)/shard_map/ppermute | solution.py:46
  11.1 10.2 %collective-permute-start.5 = (bf16[16,1024]{1,0:T(8,128)(2,1)S(1)}, bf16[16,1024]{1,0:T(8,128)(2,1)S(1)}, u32[]{:S(2)}, u32[]{:S(2)}) collective-permute-start(bf16[16,1024]{1,0:T(8,128)(2,1)S(1)} %pad_maximum_fusion.2.halo), channel_id=1, source_target_pairs={{8,16},{16,8},{9,17},{17,9},{10,18},{18,10},{11,19},{19,11},{12,20... | collective-permute-start | bytes 98312 | tf_op jit(solution)/shard_map/ppermute | solution.py:46
  13.5 9.1 %collective-permute-start.6 = (bf16[48,1024]{1,0:T(8,128)(2,1)S(1)}, bf16[48,1024]{1,0:T(8,128)(2,1)S(1)}, u32[]{:S(2)}, u32[]{:S(2)}) collective-permute-start(bf16[48,1024]{1,0:T(8,128)(2,1)S(1)} %pad_maximum_fusion), channel_id=1, source_target_pairs={{0,16},{16,0},{8,24},{24,8},{1,17},{17,1},{9,25},{25,9},{2,18},{18... | collective-permute-start | bytes 294920 | tf_op jit(solution)/shard_map/ppermute | solution.py:46
  22.7 1.0 %copy-start.4 = (bf16[8,16,1024]{2,1,0:T(8,128)(2,1)S(1)}, bf16[8,16,1024]{2,1,0:T(8,128)(2,1)}, u32[]{:S(2)}) copy-start(bf16[8,16,1024]{2,1,0:T(8,128)(2,1)} %tok.1) | copy-start | bytes 786436
  23.6 0.7 %copy-start.5 = (f32[1024]{0:T(1024)S(1)}, f32[1024]{0:T(1024)}, u32[]{:S(2)}) copy-start(f32[1024]{0:T(1024)} %param.11) | copy-start | bytes 12292
  24.3 0.7 %copy-start.6 = (f32[1024]{0:T(1024)S(1)}, f32[1024]{0:T(1024)}, u32[]{:S(2)}) copy-start(f32[1024]{0:T(1024)} %param.13) | copy-start | bytes 12292
  30.8 4.1 %collective-permute-start.10 = (bf16[128,1024]{1,0:T(8,128)(2,1)S(1)}, bf16[128,1024]{1,0:T(8,128)(2,1)S(1)}, u32[]{:S(2)}, u32[]{:S(2)}) collective-permute-start(bf16[128,1024]{1,0:T(8,128)(2,1)S(1)} %get-tuple-element.13.own), channel_id=1, source_target_pairs={{0,1},{1,0},{2,3},{3,2},{4,5},{5,4},{6,7},{7,6},{8,9},{9,8},{10,11... | collective-permute-start | bytes 786440 | tf_op jit(solution)/shard_map/ppermute | solution.py:46
  30.9 6.3 %collective-permute-start.13 = (bf16[128,1024]{1,0:T(8,128)(2,1)S(1)}, bf16[128,1024]{1,0:T(8,128)(2,1)S(1)}, u32[]{:S(2)}, u32[]{:S(2)}) collective-permute-start(bf16[128,1024]{1,0:T(8,128)(2,1)S(1)} %get-tuple-element.14.own_a), channel_id=1, source_target_pairs={{0,1},{1,0},{2,3},{3,2},{4,5},{5,4},{6,7},{7,6},{8,9},{9,8},{10,11... | collective-permute-start | bytes 786440 | tf_op jit(solution)/shard_map/ppermute | solution.py:46
  31.4 10.5 %collective-permute-start.7 = (bf16[128,1024]{1,0:T(8,128)(2,1)S(1)}, bf16[128,1024]{1,0:T(8,128)(2,1)S(1)}, u32[]{:S(2)}, u32[]{:S(2)}) collective-permute-start(bf16[128,1024]{1,0:T(8,128)(2,1)S(1)} %get-tuple-element.13.own), channel_id=1, source_target_pairs={{1,2},{2,1},{3,4},{4,3},{5,6},{6,5},{7,0},{0,7},{9,10},{10,9},{11,... | collective-permute-start | bytes 786440 | tf_op jit(solution)/shard_map/ppermute | solution.py:46
  31.7 11.0 %collective-permute-start.14 = (bf16[128,1024]{1,0:T(8,128)(2,1)S(1)}, bf16[128,1024]{1,0:T(8,128)(2,1)S(1)}, u32[]{:S(2)}, u32[]{:S(2)}) collective-permute-start(bf16[128,1024]{1,0:T(8,128)(2,1)S(1)} %get-tuple-element.15.own_b), channel_id=1, source_target_pairs={{0,1},{1,0},{2,3},{3,2},{4,5},{5,4},{6,7},{7,6},{8,9},{9,8},{10,11... | collective-permute-start | bytes 786440 | tf_op jit(solution)/shard_map/ppermute | solution.py:46
  31.7 25.3 %collective-permute-start.8 = (bf16[128,1024]{1,0:T(8,128)(2,1)S(1)}, bf16[128,1024]{1,0:T(8,128)(2,1)S(1)}, u32[]{:S(2)}, u32[]{:S(2)}) collective-permute-start(bf16[128,1024]{1,0:T(8,128)(2,1)S(1)} %get-tuple-element.14.own_a), channel_id=1, source_target_pairs={{1,2},{2,1},{3,4},{4,3},{5,6},{6,5},{7,0},{0,7},{9,10},{10,9},{11,... | collective-permute-start | bytes 786440 | tf_op jit(solution)/shard_map/ppermute | solution.py:46
  35.0 22.1 %collective-permute-start.9 = (bf16[128,1024]{1,0:T(8,128)(2,1)S(1)}, bf16[128,1024]{1,0:T(8,128)(2,1)S(1)}, u32[]{:S(2)}, u32[]{:S(2)}) collective-permute-start(bf16[128,1024]{1,0:T(8,128)(2,1)S(1)} %get-tuple-element.15.own_b), channel_id=1, source_target_pairs={{9,10},{10,9},{11,12},{12,11},{13,14},{14,13},{15,8},{8,15},{17,18... | collective-permute-start | bytes 786440 | tf_op jit(solution)/shard_map/ppermute | solution.py:46
  37.2 19.9 %collective-permute-start.11 = (bf16[128,1024]{1,0:T(8,128)(2,1)S(1)}, bf16[128,1024]{1,0:T(8,128)(2,1)S(1)}, u32[]{:S(2)}, u32[]{:S(2)}) collective-permute-start(bf16[128,1024]{1,0:T(8,128)(2,1)S(1)} %collective-permute-done.10.on), channel_id=1, source_target_pairs={{1,2},{2,1},{3,4},{4,3},{5,6},{6,5},{7,0},{0,7},{25,26},{26,25},{2... | collective-permute-start | bytes 786440 | tf_op jit(solution)/shard_map/ppermute | solution.py:46
  41.9 15.2 %collective-permute-start.12 = (bf16[128,1024]{1,0:T(8,128)(2,1)S(1)}, bf16[128,1024]{1,0:T(8,128)(2,1)S(1)}, u32[]{:S(2)}, u32[]{:S(2)}) collective-permute-start(bf16[128,1024]{1,0:T(8,128)(2,1)S(1)} %collective-permute-done.7.off), channel_id=1, source_target_pairs={{0,1},{1,0},{2,3},{3,2},{4,5},{5,4},{6,7},{7,6},{24,25},{25,24},{2... | collective-permute-start | bytes 786440 | tf_op jit(solution)/shard_map/ppermute | solution.py:46
  42.7 1.6 %copy-start.1 = (bf16[1024,1024]{1,0:T(8,128)(2,1)S(1)}, bf16[1024,1024]{1,0:T(8,128)(2,1)}, u32[]{:S(2)}) copy-start(bf16[1024,1024]{1,0:T(8,128)(2,1)} %w_value.3) | copy-start | bytes 6291460
  44.3 0.7 copy-start.7
  45.0 1.6 %copy-start.8 = (bf16[1024,1024]{1,0:T(8,128)(2,1)S(1)}, bf16[1024,1024]{1,0:T(8,128)(2,1)}, u32[]{:S(2)}) copy-start(bf16[1024,1024]{1,0:T(8,128)(2,1)} %w_query.1) | copy-start | bytes 6291460
  46.6 10.5 %copy-start.2 = (bf16[1024,1024]{1,0:T(8,128)(2,1)S(1)}, bf16[1024,1024]{1,0:T(8,128)(2,1)}, u32[]{:S(2)}) copy-start(bf16[1024,1024]{1,0:T(8,128)(2,1)} %w_value.3) | copy-start | bytes 6291460
  46.6 10.5 %copy-start.3 = (bf16[1024,1024]{1,0:T(8,128)(2,1)S(1)}, bf16[1024,1024]{1,0:T(8,128)(2,1)}, u32[]{:S(2)}) copy-start(bf16[1024,1024]{1,0:T(8,128)(2,1)} %w_out.1) | copy-start | bytes 6291460

commit v2 on v0

v2 whole, which is shorter than its diff:
```python
import functools
import math

import jax
import jax.numpy as jnp
from jax import lax
from jax.experimental import pallas as pl
from jax.experimental.pallas import tpu as pltpu
from jax.sharding import PartitionSpec as P

EPS = 1e-06
BIG = 1e30
VMEM = pl.BlockSpec(memory_space=pltpu.VMEM)
SMEM = pl.BlockSpec(memory_space=pltpu.SMEM)


def pair_swaps(count, first):
    pairs = []
    for low in range(first, count - 1, 2):
        pairs += [(low, low + 1), (low + 1, low)]
    return pairs


def lon_pairs(lats, lat_count, lon_count, off_chip):
    pairs = []
    for lat in lats:
        for low in range(1 if off_chip else 0, lon_count, 2):
            one, two = lat * lon_count + low, lat * lon_count + (low + 1) % lon_count
            pairs += [(one, two), (two, one)]
    return pairs


def two_away(count, first):
    pairs = []
    for start in range(first, count, 4):
        for low in (start, start + 1):
            if low + 2 < count:
                pairs += [(low, low + 2), (low + 2, low)]
    return pairs


def permuted(value, axis, pairs):
    if not pairs:
        return jnp.zeros_like(value)
    return lax.ppermute(value, axis, pairs)


def unit(values):
    return lax.rsqrt(jnp.mean(values * values, axis=-1, keepdims=True) + EPS)


def partner(place, count, off_chip):
    even = place % 2 == 0
    if not off_chip:
        return jnp.where(even, place + 1, place - 1)
    return jnp.where(even, jnp.where(place == 0, count - 1, place - 1), jnp.where(place == count - 1, 0, place + 1))


def band_facts():
    lats = lax.axis_size("lat")
    band = lax.axis_index("lat")
    even = band % 2 == 0
    polar = (band == 0) | (band == lats - 1)
    return band, jnp.where(even, band + 1, band - 1), jnp.where(even, band - 1, band + 1), polar


def slot_penalties(pattern, slots):
    lons = lax.axis_size("lon")
    band, band_a, band_b, polar = band_facts()
    sector = lax.axis_index("lon")
    on, off = partner(sector, lons, False), partner(sector, lons, True)
    places = [
        (band, sector), (band_a, sector), (band_b, sector),
        (band, on), (band_a, on), (band_b, on),
        (band, off), (band_a, off),
        (jnp.where(polar, band, band_b), jnp.where(polar, partner(off, lons, False), off)),
        (jnp.where(polar, band, band_b), jnp.where(polar, partner(on, lons, True), sector)),
    ]
    exists = {2: ~polar, 5: ~polar}
    out = []
    for slot in slots:
        tile = places[slot][0] * lons + places[slot][1]
        listed = pattern[0] == tile
        for index in range(1, pattern.shape[0]):
            listed = listed | (pattern[index] == tile)
        if slot in exists:
            listed = listed & exists[slot]
        out.append(jnp.where(listed, 0.0, BIG).astype(jnp.float32))
    return out


def prep_kernel(tok, tok_out, edges, brink):
    rows, cols, width = tok.shape
    tok_out[...] = tok[...]
    first = lax.broadcasted_iota(jnp.int32, (2 * rows, width), 0)
    out = jnp.zeros((2 * rows, width), jnp.float32)
    for row in range(rows):
        line = tok[row].astype(jnp.float32)
        out = jnp.where(first == row, line[0:1], out)
        out = jnp.where(first == rows + row, line[cols - 1 : cols], out)
    edges[...] = out.astype(edges.dtype)
    brink[:cols, :] = tok[0]
    brink[cols:, :] = tok[rows - 1]


def conv_kernel(
    tok, tile_a, tile_b, halo, halo_a, halo_b, ring_a, ring_b, gains,
    hidden, second, second_a, second_b, before, middle, after, mixed,
):
    rows, cols, width = tok.shape
    gain_one, gain_two = gains[0:1, :], gains[1:2, :]
    place = lax.broadcasted_iota(jnp.int32, (cols, width), 0)

    def normed(raw):
        wide = raw.astype(jnp.float32)
        return (wide * unit(wide) * gain_one).astype(jnp.bfloat16).astype(jnp.float32)

    def put(row, value, left, right):
        middle[row] = value
        before[row] = jnp.where(place == 0, left, pltpu.roll(value, 1, 0))
        after[row] = jnp.where(place == cols - 1, right, pltpu.roll(value, cols - 1, 0))

    def tile_rows(base, raw, edges):
        sides = normed(edges[...])
        for row in range(rows):
            put(base + row, normed(raw[row]), sides[row : row + 1], sides[rows + row : rows + row + 1])

    def ring(row, data, bottom):
        base = pl.multiple_of(bottom * cols, cols)
        sides = normed(data[2 * cols :, :])
        left = jnp.where(bottom > 0, sides[rows - 1 : rows], sides[0:1])
        right = jnp.where(bottom > 0, sides[2 * rows - 1 : 2 * rows], sides[rows : rows + 1])
        put(row, normed(data[pl.ds(base, cols), :]), left, right)

    band = lax.axis_index("lat")
    odd = band % 2
    high = (band // 2) % 2
    base_own = 1 + rows
    base_a = jnp.where(odd > 0, 1, 1 + 2 * rows)
    base_b = jnp.where(odd > 0, 1 + 2 * rows, 1)
    last_row = 1 + 3 * rows
    tile_rows(base_own, tok, halo)
    tile_rows(base_a, tile_a, halo_a)
    tile_rows(base_b, tile_b, halo_b)
    ring(jnp.where(high > 0, 0, last_row), ring_a, high)
    ring(jnp.where(high > 0, last_row, 0), ring_b, 1 - high)

    for base, raw, out, keep in (
        (base_own, tok, second, True), (base_a, tile_a, second_a, False), (base_b, tile_b, second_b, False),
    ):
        for start in range(0, width, 256):
            lanes = slice(start, start + 256)
            taps = [gains[2 + index : 3 + index, lanes] for index in range(9)]
            totals = [None] * rows
            for row in range(-1, rows + 1):
                parts = [ref[base + row, :, lanes] for ref in (before, middle, after)]
                for target in range(max(row - 1, 0), min(row + 2, rows)):
                    for along in range(3):
                        term = parts[along] * taps[3 * (row - target + 1) + along]
                        totals[target] = term if totals[target] is None else totals[target] + term
            for row in range(rows):
                mixed[row * cols : (row + 1) * cols, lanes] = (
                    raw[row, :, lanes].astype(jnp.float32) + totals[row]
                ).astype(jnp.bfloat16)
        if keep:
            hidden[...] = mixed[...]
        for row in range(rows):
            at = slice(row * cols, (row + 1) * cols)
            wide = mixed[at, :].astype(jnp.float32)
            out[at, :] = (wide * unit(wide) * gain_two).astype(jnp.bfloat16)


def head_marks(model, head):
    channel = lax.broadcasted_iota(jnp.int32, (model, 128), 0) // head
    index = lax.broadcasted_iota(jnp.int32, (model, 128), 1) % 64
    return jnp.where(channel == index, 1.0, 0.0).astype(jnp.bfloat16)


def head_units(wide, marks, head):
    square = (wide * wide).astype(jnp.bfloat16)
    total = jnp.dot(square, marks, preferred_element_type=jnp.float32)
    share = lax.rsqrt(total * (1.0 / head) + EPS)
    high = share.astype(jnp.bfloat16).astype(jnp.float32)
    lane = lax.broadcasted_iota(jnp.int32, share.shape, 1)
    split = jnp.where(lane < 64, high, share - high).astype(jnp.bfloat16)
    factor = lax.dot_general(
        split, marks, (((1,), (1,)), ((), ())), preferred_element_type=jnp.float32
    )
    return (wide * factor).astype(jnp.bfloat16)


CHUNK = 256


def group_kernel(heads, slots, first, last, *refs):
    refs = list(refs)

    def take(count):
        out = refs[:count]
        del refs[:count]
        return out

    pattern, scale_in = take(2)
    tiles = take(len(slots) + last)
    w_key, w_value = take(2)
    if first:
        (w_query,) = take(1)
    else:
        queries, tops, lows, sums = take(4)
    if last:
        w_out, hidden, result = take(3)
    else:
        if first:
            (queries,) = take(1)
        tops_out, lows_out, sums_out = take(3)
    keys, values = take(2)
    if last:
        (joined,) = take(1)

    size, model = tiles[0].shape
    head = model // heads
    width = 2 * head
    marks = head_marks(model, head)
    if first:
        raw = jnp.dot(tiles[0][...], w_query[...], preferred_element_type=jnp.float32)
        queries[...] = head_units(raw, marks, head)
    tokens = [ref[...] for ref in tiles]
    if last:
        other = tokens.pop()
        tokens[-1] = jnp.where(band_facts()[3], tokens[-1], other)
    tokens = jnp.concatenate(tokens, axis=0)
    raw = jnp.dot(tokens, w_key[...], preferred_element_type=jnp.float32)
    keys[...] = head_units(raw, marks, head)
    values[...] = lax.dot_general(
        w_value[...], tokens, (((1,), (1,)), ((), ())), preferred_element_type=jnp.float32
    ).astype(jnp.bfloat16)

    flags = slot_penalties(pattern, slots)
    factor = math.log2(math.e) / math.sqrt(head)
    lane = lax.broadcasted_iota(jnp.int32, (size, width), 1)
    half = lax.broadcasted_iota(jnp.int32, (1, 2 * size), 1) < size
    for pair in range(heads // 2):
        lanes = slice(pair * width, (pair + 1) * width)
        query = queries[:, lanes]
        zero = jnp.zeros_like(query)
        both = jnp.concatenate(
            [jnp.where(lane < head, query, zero), jnp.where(lane < head, zero, query)], axis=0
        )
        scores = lax.dot_general(
            keys[:, lanes], both, (((1,), (1,)), ((), ())), preferred_element_type=jnp.float32
        )
        scale = jnp.where(half, scale_in[2 * pair] * factor, scale_in[2 * pair + 1] * factor)
        parts = [scores[slot * size : (slot + 1) * size] * scale for slot in range(len(slots))]
        best = None if first else tops[pair : pair + 1, :]
        for part, flag in zip(parts, flags):
            peak = jnp.max(part, axis=0, keepdims=True) - flag
            best = peak if best is None else jnp.maximum(best, peak)
        exps = [jnp.exp2(part - (best + flag)) for part, flag in zip(parts, flags)]
        total = exps[0]
        for part in exps[1:]:
            total = total + part
        low = jnp.sum(total, axis=0, keepdims=True)
        weights = jnp.concatenate([part.astype(jnp.bfloat16) for part in exps], axis=0)
        mixed = jnp.dot(values[lanes, :], weights, preferred_element_type=jnp.float32)
        mixed = jnp.concatenate([mixed[:head, :size], mixed[head:, size:]], axis=0)
        if not first:
            old = jnp.exp2(tops[pair : pair + 1, :] - best)
            low = low + old * lows[pair : pair + 1, :]
            mixed = mixed + sums[lanes, :] * spans(old, size, head)
        if last:
            joined[:, lanes] = jnp.transpose(mixed * spans(1.0 / low, size, head)).astype(jnp.bfloat16)
        else:
            sums_out[lanes, :] = mixed
            tops_out[pair : pair + 1, :] = best
            lows_out[pair : pair + 1, :] = low
    if not last:
        return
    attended = joined[...]
    for start in range(0, model, CHUNK):
        part = slice(start, start + CHUNK)
        out = jnp.dot(attended, w_out[:, part], preferred_element_type=jnp.float32)
        result[:, part] = (hidden[:, part].astype(jnp.float32) + out).astype(jnp.bfloat16)


def spans(row, size, head):
    return jnp.concatenate(
        [jnp.broadcast_to(row[:, :size], (head, size)), jnp.broadcast_to(row[:, size:], (head, size))],
        axis=0,
    )


def limit(mebibytes):
    return pltpu.CompilerParams(vmem_limit_bytes=mebibytes * 2**20)


def attend(heads, slots, pattern, scale, tiles, weights, state, finish):
    first, last = state is None, finish is not None
    size, model = tiles[0].shape
    tile = jax.ShapeDtypeStruct((size, model), jnp.bfloat16)
    stats = jax.ShapeDtypeStruct((heads // 2, 2 * size), jnp.float32)
    out = [stats, stats, jax.ShapeDtypeStruct((model, size), jnp.float32)]
    if last:
        out = [tile]
    elif first:
        out = [tile] + out
    operands = [pattern, scale, *tiles, *weights]
    if not first:
        operands += list(state)
    if last:
        operands += list(finish)
    scratch = [
        pltpu.VMEM((len(slots) * size, model), jnp.bfloat16),
        pltpu.VMEM((model, len(slots) * size), jnp.bfloat16),
    ]
    if last:
        scratch.append(pltpu.VMEM((size, model), jnp.bfloat16))
    return pl.pallas_call(
        functools.partial(group_kernel, heads, slots, first, last),
        out_shape=out,
        in_specs=[SMEM, SMEM] + [VMEM] * (len(operands) - 2),
        out_specs=[VMEM] * len(out),
        scratch_shapes=scratch,
        compiler_params=limit(16),
        cost_estimate=pl.CostEstimate(
            flops=2**36, bytes_accessed=2**28, transcendentals=0
        ),
        name="attend" + "_".join(str(slot) for slot in slots),
    )(*operands)


def on_device(
    tokens, norm1_gain, conv_weight, norm2_gain, w_query, w_key, w_value, w_out, head_scale, pattern
):
    rows, cols, model = tokens.shape
    size = rows * cols
    heads = head_scale.shape[0]
    lats, lons = lax.axis_size("lat"), lax.axis_size("lon")
    polar = band_facts()[3]
    even_sector = lax.axis_index("lon") % 2 == 0
    lists = pattern.reshape(-1)

    swap_a = functools.partial(permuted, axis="lat", pairs=pair_swaps(lats, 0))
    swap_b = functools.partial(permuted, axis="lat", pairs=pair_swaps(lats, 1))

    def across(value, off_chip):
        return permuted(value, ("lat", "lon"), lon_pairs(range(lats), lats, lons, off_chip))

    tile_a, tile_b = swap_a(tokens), swap_b(tokens)
    tok, edges, brink = pl.pallas_call(
        prep_kernel,
        out_shape=[
            jax.ShapeDtypeStruct(shape, tokens.dtype)
            for shape in (tokens.shape, (2 * rows, model), (2 * cols, model))
        ],
        in_specs=[VMEM],
        out_specs=[VMEM] * 3,
        compiler_params=limit(2),
        cost_estimate=pl.CostEstimate(flops=0, bytes_accessed=2**21, transcendentals=0),
        name="prep",
    )(tokens)
    gains = jnp.concatenate(
        [norm1_gain.reshape(1, model), norm2_gain.reshape(1, model), conv_weight.reshape(9, model)],
        axis=0,
    )
    on_edges, off_edges = across(edges, False), across(edges, True)
    halo = jnp.concatenate(
        [
            jnp.where(even_sector, off_edges[rows:], on_edges[rows:]),
            jnp.where(even_sector, on_edges[:rows], off_edges[:rows]),
        ],
        axis=0,
    )
    halo_a, halo_b = swap_a(halo), swap_b(halo)
    brink = jnp.concatenate([brink, halo], axis=0)
    ring_a = permuted(brink, "lat", two_away(lats, 0))
    ring_b = permuted(brink, "lat", two_away(lats, 2))

    tile = jax.ShapeDtypeStruct((size, model), jnp.bfloat16)
    w_value = jnp.transpose(w_value)
    gains, w_value = lax.optimization_barrier((gains, w_value))
    window = pltpu.VMEM((2 + 3 * rows, cols, model), jnp.float32)
    hidden, second, second_a, second_b = pl.pallas_call(
        conv_kernel,
        out_shape=[tile] * 4,
        in_specs=[VMEM] * 9,
        out_specs=[VMEM] * 4,
        scratch_shapes=[window] * 3 + [pltpu.VMEM((size, model), jnp.bfloat16)],
        compiler_params=limit(10),
        cost_estimate=pl.CostEstimate(flops=2**24, bytes_accessed=24 * 2**20, transcendentals=0),
        name="conv",
    )(
        tok, tile_a, tile_b, halo, halo_a, halo_b, ring_a, ring_b, gains
    )

    on = across(second, False)
    off = across(second, True)
    on_a, on_b = across(second_a, False), across(second_b, False)
    off_a = across(second_a, True)
    third = across(jnp.where(polar, on, second_b), True)

    queries, *state = attend(
        heads, (0, 1, 3, 4, 5), lists, head_scale, [second, second_a, on, on_a, on_b],
        [w_key, w_value, w_query], None, None,
    )
    off, queries = lax.optimization_barrier((off, queries))
    on_y = across(off, False)
    (result,) = attend(
        heads, (6, 7, 8, 9), lists, head_scale, [off, off_a, third, on_y, second_b], [w_key, w_value],
        [queries, *state], [w_out, hidden],
    )
    return result.reshape(rows, cols, model)


def solution(mesh):
    return jax.shard_map(
        on_device,
        mesh=mesh,
        in_specs=(
            P("lat", "lon", None),
            P(),
            P(),
            P(),
            P(),
            P(),
            P(),
            P(),
            P(),
            P("lat", "lon", None),
        ),
        out_specs=P("lat", "lon", None),
        check_vma=False,
    )
```

time: 146 us -> 56.1 us (0.38)
  the two profiles are of different devices: /device:TPU:14 before, /device:TPU:2 now
where the time goes in v2:
time: 56.1 us; the launch traced here: 55.7 us
  Pallas kernels  21.5 us (38%)
  starting transfers between devices  15.5 us (28%)
  waiting for transfers between devices  10.3 us (18%)
  local copies, waits for them, and re-layouts  7.6 us (14%)
  other arithmetic  0.78 us (1%)
    pallas_call x2, Pallas kernels, attend(): pl.pallas_call(functools.partial(group_kernel, heads, slots, first, last)...  17.2 us
    ppermute x14, starting transfers between devices, permuted(): return lax.ppermute(value, axis, pairs)  15.5 us
    ppermute x14, waiting for transfers between devices, permuted(): return lax.ppermute(value, axis, pairs)  10.3 us
    unnamed x15, local copies, waits for them, and re-layouts  6.77 us
    pallas_call x1, Pallas kernels, on_device(): pl.pallas_call(conv_kernel, out_shape=[tile] * 4, in_specs=[VMEM] * 9, ou...  3.22 us
  transfers between devices with their start and end apart: 14, of which 4 were waited for; matrix products, arithmetic and copies ran while one was open for 8% of the time, Pallas kernels for 16%

profile of v2, /device:TPU:2, one launch (start us, length us, event | category | flops | bytes accessed | tf_op | source)
XLA Modules:
  0.0 55.7 jit_solution(8332372580982488441)
XLA Ops:
  0.0 1.0 %prep.1 = (bf16[8,16,1024]{2,1,0:T(8,128)(2,1)S(1)}, bf16[16,1024]{1,0:T(8,128)(2,1)S(1)}, bf16[32,1024]{1,0:T(8,128)(2,1)S(1)}) custom-call(bf16[8,16,1024]{2,1,0:T(8,128)(2,1)} %tok.1), custom_call_target="tpu_custom_call" | custom-call | bytes 2097152 | tf_op jit(solution)/shard_map/prep/pallas_call | solution.py:349
  1.0 3.1 %collective-permute-start.2 = (bf16[16,1024]{1,0:T(8,128)(2,1)S(1)}, bf16[16,1024]{1,0:T(8,128)(2,1)S(1)}, u32[]{:S(2)}, u32[]{:S(2)}) collective-permute-start(bf16[16,1024]{1,0:T(8,128)(2,1)S(1)} %get-tuple-element.21), channel_id=1, source_target_pairs={{1,2},{2,1},{3,4},{4,3},{5,6},{6,5},{7,0},{0,7},{9,10},{10,9},{11,... | collective-permute-start | bytes 98312 | tf_op jit(solution)/shard_map/ppermute | solution.py:45
  4.1 0.0 collective-permute-start.3
  4.1 0.5 collective-permute-start
  4.7 4.3 %collective-permute-start.1 = (bf16[8,16,1024]{2,1,0:T(8,128)(2,1)}, bf16[8,16,1024]{2,1,0:T(8,128)(2,1)S(1)}, u32[]{:S(2)}, u32[]{:S(2)}) collective-permute-start(bf16[8,16,1024]{2,1,0:T(8,128)(2,1)} %tok.1), channel_id=1, source_target_pairs={{8,16},{16,8},{9,17},{17,9},{10,18},{18,10},{11,19},{19,11},{12,20... | collective-permute-start | bytes 786440 | tf_op jit(solution)/shard_map/ppermute | solution.py:45
  9.0 0.8 %reshape.18 = f32[9,1024]{1,0:T(8,128)S(1)} reshape(f32[3,3,1024]{2,1,0:T(4,128)} %param.12) | data formatting | bytes 73728 | tf_op jit(solution)/shard_map/reshape | solution.py:362
  9.9 0.0 collective-permute-done.2
  9.9 0.0 collective-permute-done.3
  9.9 0.1 collective-permute-start.4
  10.0 2.4 %collective-permute-start.5 = (bf16[16,1024]{1,0:T(8,128)(2,1)S(1)}, bf16[16,1024]{1,0:T(8,128)(2,1)S(1)}, u32[]{:S(2)}, u32[]{:S(2)}) collective-permute-start(bf16[16,1024]{1,0:T(8,128)(2,1)S(1)} %pad_maximum_fusion.2.halo), channel_id=1, source_target_pairs={{8,16},{16,8},{9,17},{17,9},{10,18},{18,10},{11,19},{19,11},{12,20... | collective-permute-start | bytes 98312 | tf_op jit(solution)/shard_map/ppermute | solution.py:45
  12.4 0.1 collective-permute-start.6
  12.5 0.7 %pad_maximum_fusion.1.gains = f32[11,1024]{1,0:T(8,128)S(1)} fusion(f32[9,1024]{1,0:T(8,128)S(1)} %reshape.18, f32[1,1024]{1,0:T(1,128)} %bitcast.9, f32[1,1024]{1,0:T(1,128)} %bitcast.10), kind=kLoop, calls=%fused_computation.2 | loop fusion | flops 22528 | bytes 90112 | tf_op jit(solution)/shard_map/concatenate | solution.py:361
  13.2 0.0 copy-start.5
  13.2 0.0 copy-start.6
  13.2 2.9 %copy.11 = bf16[1024,1024]{0,1:T(8,128)(2,1)S(1)} copy(bf16[1024,1024]{1,0:T(8,128)(2,1)} %param.16) | data formatting | bytes 4194304 | tf_op args[6]
  16.1 1.8 %collective-permute-done.4.halo_a = bf16[16,1024]{1,0:T(8,128)(2,1)S(1)} collective-permute-done((bf16[16,1024]{1,0:T(8,128)(2,1)S(1)}, bf16[16,1024]{1,0:T(8,128)(2,1)S(1)}, u32[]{:S(2)}, u32[]{:S(2)}) %collective-permute-start.4) | collective-permute-done | bytes 32800 | tf_op jit(solution)/shard_map/ppermute | solution.py:45
  17.9 3.3 %collective-permute-done.5.halo_b = bf16[16,1024]{1,0:T(8,128)(2,1)S(1)} collective-permute-done((bf16[16,1024]{1,0:T(8,128)(2,1)S(1)}, bf16[16,1024]{1,0:T(8,128)(2,1)S(1)}, u32[]{:S(2)}, u32[]{:S(2)}) %collective-permute-start.5) | collective-permute-done | bytes 32800 | tf_op jit(solution)/shard_map/ppermute | solution.py:45
  21.1 1.3 %collective-permute-done.6.ring_a = bf16[48,1024]{1,0:T(8,128)(2,1)S(1)} collective-permute-done((bf16[48,1024]{1,0:T(8,128)(2,1)S(1)}, bf16[48,1024]{1,0:T(8,128)(2,1)S(1)}, u32[]{:S(2)}, u32[]{:S(2)}) %collective-permute-start.6) | collective-permute-done | bytes 98336 | tf_op jit(solution)/shard_map/ppermute | solution.py:45
  22.4 0.0 collective-permute-done.tile_a
  22.4 0.0 collective-permute-done.1.tile_b
  22.5 3.2 %conv.1 = (bf16[128,1024]{1,0:T(8,128)(2,1)S(1)}, bf16[128,1024]{1,0:T(8,128)(2,1)}, bf16[128,1024]{1,0:T(8,128)(2,1)}, bf16[128,1024]{1,0:T(8,128)(2,1)S(1)}) custom-call(bf16[8,16,1024]{2,1,0:T(8,128)(2,1)S(1)} %get-tuple-element.20.tok, bf16[8,16,1024]{2,1,0:T(8,128)(2,1)S(1)} %collective-permute-done.tile_a, ...), custom_call_target="tpu_custom_call" | custom-call | flops 16777216 | bytes 25165824 | tf_op jit(solution)/shard_map/conv/pallas_call | solution.py:382
  25.7 0.0 copy-start.3
  25.7 0.7 %copy-done.3 = bf16[128,1024]{1,0:T(8,128)(2,1)} copy-done((bf16[128,1024]{1,0:T(8,128)(2,1)}, bf16[128,1024]{1,0:T(8,128)(2,1)S(1)}, u32[]{:S(2)}) %copy-start.3) | copy-done | bytes 262168
  26.4 0.0 collective-permute-start.8
  26.4 0.5 collective-permute-start.10
  26.9 0.0 collective-permute-start.9
  26.9 0.7 %collective-permute-start.7 = (bf16[128,1024]{1,0:T(8,128)(2,1)}, bf16[128,1024]{1,0:T(8,128)(2,1)S(1)}, u32[]{:S(2)}, u32[]{:S(2)}) collective-permute-start(bf16[128,1024]{1,0:T(8,128)(2,1)} %get-tuple-element.24.refs_2_), channel_id=1, source_target_pairs={{1,2},{2,1},{3,4},{4,3},{5,6},{6,5},{7,0},{0,7},{9,10},{10,9},{11,... | collective-permute-start | bytes 786440 | tf_op jit(solution)/shard_map/ppermute | solution.py:45
  27.7 2.8 %collective-permute-start.11 = (bf16[128,1024]{1,0:T(8,128)(2,1)}, bf16[128,1024]{1,0:T(8,128)(2,1)S(1)}, u32[]{:S(2)}, u32[]{:S(2)}) collective-permute-start(bf16[128,1024]{1,0:T(8,128)(2,1)} %get-tuple-element.25.refs_3_), channel_id=1, source_target_pairs={{1,2},{2,1},{3,4},{4,3},{5,6},{6,5},{7,0},{0,7},{9,10},{10,9},{11,... | collective-permute-start | bytes 786440 | tf_op jit(solution)/shard_map/ppermute | solution.py:45
  30.5 0.0 collective-permute-done.8.refs_4_
  30.5 0.8 %collective-permute-start.12 = (bf16[128,1024]{1,0:T(8,128)(2,1)S(1)}, bf16[128,1024]{1,0:T(8,128)(2,1)S(1)}, u32[]{:S(2)}, u32[]{:S(2)}) collective-permute-start(bf16[128,1024]{1,0:T(8,128)(2,1)S(1)} %broadcast_select_fusion), channel_id=1, source_target_pairs={{1,2},{2,1},{3,4},{4,3},{5,6},{6,5},{7,0},{0,7},{9,10},{10,9},{11,... | collective-permute-start | bytes 786440 | tf_op jit(solution)/shard_map/ppermute | solution.py:45
  31.3 0.0 collective-permute-done.10.refs_6_
  31.3 0.0 collective-permute-done.9.refs_5_
  31.3 0.0 copy-done.5
  31.3 0.0 copy-done.6
  31.3 0.0 copy-start
  31.3 1.6 %copy-done = bf16[1024,1024]{1,0:T(8,128)(2,1)S(1)} copy-done((bf16[1024,1024]{1,0:T(8,128)(2,1)S(1)}, bf16[1024,1024]{1,0:T(8,128)(2,1)}, u32[]{:S(2)}) %copy-start) | copy-done | bytes 2097176
  32.9 0.0 copy-start.1
  32.9 1.6 %copy-done.1 = bf16[1024,1024]{1,0:T(8,128)(2,1)S(1)} copy-done((bf16[1024,1024]{1,0:T(8,128)(2,1)S(1)}, bf16[1024,1024]{1,0:T(8,128)(2,1)}, u32[]{:S(2)}) %copy-start.1) | copy-done | bytes 2097176
  34.5 0.0 copy-start.2
  34.5 9.2 %attend0_1_3_4_5.1 = (bf16[128,1024]{1,0:T(8,128)(2,1)S(1)}, f32[8,256]{1,0:T(8,128)S(1)}, f32[8,256]{1,0:T(8,128)S(1)}, f32[1024,128]{1,0:T(8,128)S(1)}) custom-call(s32[8]{0:T(128)S(1)} %bitcast.7, f32[16]{0:T(128)S(1)} %copy-done.6, bf16[128,1024]{1,0:T(8,128)(2,1)} %get-tuple-element.24.refs_2_, bf16[128,1024]{1,0:T(8,128)(2,1)} %get-tuple-element.25.refs_3_, ...), custom_call_target="tpu_custom_call" | custom-call | flops 68719476736 | bytes 268435456 | tf_op jit(solution)/shard_map/attend0_1_3_4_5/pallas_call | solution.py:317
  43.7 0.0 collective-permute-done.7.refs_2_
  43.7 0.1 collective-permute-start.13
  43.8 0.0 collective-permute-done.11.refs_3_
  43.8 3.9 %collective-permute-done.12.refs_4_ = bf16[128,1024]{1,0:T(8,128)(2,1)S(1)} collective-permute-done((bf16[128,1024]{1,0:T(8,128)(2,1)S(1)}, bf16[128,1024]{1,0:T(8,128)(2,1)S(1)}, u32[]{:S(2)}, u32[]{:S(2)}) %collective-permute-start.12) | collective-permute-done | bytes 262176 | tf_op jit(solution)/shard_map/ppermute | solution.py:45
  47.7 0.0 collective-permute-done.13.refs_5_
  47.7 0.0 copy-done.2
  47.7 0.0 copy-done.4
  47.7 8.0 %attend6_7_8_9.1 = bf16[128,1024]{1,0:T(8,128)(2,1)} custom-call(s32[8]{0:T(128)S(1)} %bitcast.8, f32[16]{0:T(128)S(1)} %copy-done.6, bf16[128,1024]{1,0:T(8,128)(2,1)S(1)} %collective-permute-done.7.refs_2_, bf16[128,1024]{1,0:T(8,128)(2,1)S(1)} %collective-permute-done.11.refs_3_, bf16[128,1024]{1,0:T(8,128)(2,1)S(1)} %collective-permute-done.12.refs_4_, ...), custom_call_target="tpu_custom_call" | custom-call | flops 68719476736 | bytes 268435456 | tf_op jit(solution)/shard_map/attend6_7_8_9/pallas_call | solution.py:317
  (6 shorter events, 0.1 us)
Async XLA Ops:
  1.0 8.8 %collective-permute-start.2 = (bf16[16,1024]{1,0:T(8,128)(2,1)S(1)}, bf16[16,1024]{1,0:T(8,128)(2,1)S(1)}, u32[]{:S(2)}, u32[]{:S(2)}) collective-permute-start(bf16[16,1024]{1,0:T(8,128)(2,1)S(1)} %get-tuple-element.21), channel_id=1, source_target_pairs={{1,2},{2,1},{3,4},{4,3},{5,6},{6,5},{7,0},{0,7},{9,10},{10,9},{11,... | collective-permute-start | bytes 98312 | tf_op jit(solution)/shard_map/ppermute | solution.py:45
  4.1 5.7 %collective-permute-start.3 = (bf16[16,1024]{1,0:T(8,128)(2,1)S(1)}, bf16[16,1024]{1,0:T(8,128)(2,1)S(1)}, u32[]{:S(2)}, u32[]{:S(2)}) collective-permute-start(bf16[16,1024]{1,0:T(8,128)(2,1)S(1)} %get-tuple-element.21), channel_id=1, source_target_pairs={{0,1},{1,0},{2,3},{3,2},{4,5},{5,4},{6,7},{7,6},{8,9},{9,8},{10,11... | collective-permute-start | bytes 98312 | tf_op jit(solution)/shard_map/ppermute | solution.py:45
  4.1 18.3 %collective-permute-start = (bf16[8,16,1024]{2,1,0:T(8,128)(2,1)}, bf16[8,16,1024]{2,1,0:T(8,128)(2,1)S(1)}, u32[]{:S(2)}, u32[]{:S(2)}) collective-permute-start(bf16[8,16,1024]{2,1,0:T(8,128)(2,1)} %tok.1), channel_id=1, source_target_pairs={{0,8},{8,0},{16,24},{24,16},{1,9},{9,1},{17,25},{25,17},{2,10},{10... | collective-permute-start | bytes 786440 | tf_op jit(solution)/shard_map/ppermute | solution.py:45
  4.7 17.8 %collective-permute-start.1 = (bf16[8,16,1024]{2,1,0:T(8,128)(2,1)}, bf16[8,16,1024]{2,1,0:T(8,128)(2,1)S(1)}, u32[]{:S(2)}, u32[]{:S(2)}) collective-permute-start(bf16[8,16,1024]{2,1,0:T(8,128)(2,1)} %tok.1), channel_id=1, source_target_pairs={{8,16},{16,8},{9,17},{17,9},{10,18},{18,10},{11,19},{19,11},{12,20... | collective-permute-start | bytes 786440 | tf_op jit(solution)/shard_map/ppermute | solution.py:45
  9.9 8.0 %collective-permute-start.4 = (bf16[16,1024]{1,0:T(8,128)(2,1)S(1)}, bf16[16,1024]{1,0:T(8,128)(2,1)S(1)}, u32[]{:S(2)}, u32[]{:S(2)}) collective-permute-start(bf16[16,1024]{1,0:T(8,128)(2,1)S(1)} %pad_maximum_fusion.2.halo), channel_id=1, source_target_pairs={{0,8},{8,0},{16,24},{24,16},{1,9},{9,1},{17,25},{25,17},{2,10},{10... | collective-permute-start | bytes 98312 | tf_op jit(solution)/shard_map/ppermute | solution.py:45
  10.0 11.1 %collective-permute-start.5 = (bf16[16,1024]{1,0:T(8,128)(2,1)S(1)}, bf16[16,1024]{1,0:T(8,128)(2,1)S(1)}, u32[]{:S(2)}, u32[]{:S(2)}) collective-permute-start(bf16[16,1024]{1,0:T(8,128)(2,1)S(1)} %pad_maximum_fusion.2.halo), channel_id=1, source_target_pairs={{8,16},{16,8},{9,17},{17,9},{10,18},{18,10},{11,19},{19,11},{12,20... | collective-permute-start | bytes 98312 | tf_op jit(solution)/shard_map/ppermute | solution.py:45
  12.4 10.0 %collective-permute-start.6 = (bf16[48,1024]{1,0:T(8,128)(2,1)S(1)}, bf16[48,1024]{1,0:T(8,128)(2,1)S(1)}, u32[]{:S(2)}, u32[]{:S(2)}) collective-permute-start(bf16[48,1024]{1,0:T(8,128)(2,1)S(1)} %pad_maximum_fusion), channel_id=1, source_target_pairs={{0,16},{16,0},{8,24},{24,8},{1,17},{17,1},{9,25},{25,9},{2,18},{18... | collective-permute-start | bytes 294920 | tf_op jit(solution)/shard_map/ppermute | solution.py:45
  13.2 18.1 %copy-start.5 = (s32[1,1,8]{2,1,0:T(1,128)S(1)}, s32[1,1,8]{2,1,0:T(1,128)}, u32[]{:S(2)}) copy-start(s32[1,1,8]{2,1,0:T(1,128)} %param.19) | copy-start | bytes 100
  13.2 18.1 %copy-start.6 = (f32[16]{0:T(128)S(1)}, f32[16]{0:T(128)}, u32[]{:S(2)}) copy-start(f32[16]{0:T(128)} %refs_1_.3) | copy-start | bytes 196
  25.7 0.7 %copy-start.3 = (bf16[128,1024]{1,0:T(8,128)(2,1)}, bf16[128,1024]{1,0:T(8,128)(2,1)S(1)}, u32[]{:S(2)}) copy-start(bf16[128,1024]{1,0:T(8,128)(2,1)S(1)} %get-tuple-element.34.refs_14_) | copy-start | bytes 786436
  26.4 4.1 %collective-permute-start.8 = (bf16[128,1024]{1,0:T(8,128)(2,1)}, bf16[128,1024]{1,0:T(8,128)(2,1)S(1)}, u32[]{:S(2)}, u32[]{:S(2)}) collective-permute-start(bf16[128,1024]{1,0:T(8,128)(2,1)} %get-tuple-element.24.refs_2_), channel_id=1, source_target_pairs={{0,1},{1,0},{2,3},{3,2},{4,5},{5,4},{6,7},{7,6},{8,9},{9,8},{10,11... | collective-permute-start | bytes 786440 | tf_op jit(solution)/shard_map/ppermute | solution.py:45
  26.4 4.9 %collective-permute-start.10 = (bf16[128,1024]{1,0:T(8,128)(2,1)S(1)}, bf16[128,1024]{1,0:T(8,128)(2,1)S(1)}, u32[]{:S(2)}, u32[]{:S(2)}) collective-permute-start(bf16[128,1024]{1,0:T(8,128)(2,1)S(1)} %get-tuple-element.26.refs_6_), channel_id=1, source_target_pairs={{0,1},{1,0},{2,3},{3,2},{4,5},{5,4},{6,7},{7,6},{8,9},{9,8},{10,11... | collective-permute-start | bytes 786440 | tf_op jit(solution)/shard_map/ppermute | solution.py:45
  26.9 4.4 %collective-permute-start.9 = (bf16[128,1024]{1,0:T(8,128)(2,1)}, bf16[128,1024]{1,0:T(8,128)(2,1)S(1)}, u32[]{:S(2)}, u32[]{:S(2)}) collective-permute-start(bf16[128,1024]{1,0:T(8,128)(2,1)} %get-tuple-element.25.refs_3_), channel_id=1, source_target_pairs={{0,1},{1,0},{2,3},{3,2},{4,5},{5,4},{6,7},{7,6},{8,9},{9,8},{10,11... | collective-permute-start | bytes 786440 | tf_op jit(solution)/shard_map/ppermute | solution.py:45
  26.9 16.8 %collective-permute-start.7 = (bf16[128,1024]{1,0:T(8,128)(2,1)}, bf16[128,1024]{1,0:T(8,128)(2,1)S(1)}, u32[]{:S(2)}, u32[]{:S(2)}) collective-permute-start(bf16[128,1024]{1,0:T(8,128)(2,1)} %get-tuple-element.24.refs_2_), channel_id=1, source_target_pairs={{1,2},{2,1},{3,4},{4,3},{5,6},{6,5},{7,0},{0,7},{9,10},{10,9},{11,... | collective-permute-start | bytes 786440 | tf_op jit(solution)/shard_map/ppermute | solution.py:45
  27.7 16.1 %collective-permute-start.11 = (bf16[128,1024]{1,0:T(8,128)(2,1)}, bf16[128,1024]{1,0:T(8,128)(2,1)S(1)}, u32[]{:S(2)}, u32[]{:S(2)}) collective-permute-start(bf16[128,1024]{1,0:T(8,128)(2,1)} %get-tuple-element.25.refs_3_), channel_id=1, source_target_pairs={{1,2},{2,1},{3,4},{4,3},{5,6},{6,5},{7,0},{0,7},{9,10},{10,9},{11,... | collective-permute-start | bytes 786440 | tf_op jit(solution)/shard_map/ppermute | solution.py:45
  30.5 17.2 %collective-permute-start.12 = (bf16[128,1024]{1,0:T(8,128)(2,1)S(1)}, bf16[128,1024]{1,0:T(8,128)(2,1)S(1)}, u32[]{:S(2)}, u32[]{:S(2)}) collective-permute-start(bf16[128,1024]{1,0:T(8,128)(2,1)S(1)} %broadcast_select_fusion), channel_id=1, source_target_pairs={{1,2},{2,1},{3,4},{4,3},{5,6},{6,5},{7,0},{0,7},{9,10},{10,9},{11,... | collective-permute-start | bytes 786440 | tf_op jit(solution)/shard_map/ppermute | solution.py:45
  31.3 1.6 %copy-start = (bf16[1024,1024]{1,0:T(8,128)(2,1)S(1)}, bf16[1024,1024]{1,0:T(8,128)(2,1)}, u32[]{:S(2)}) copy-start(bf16[1024,1024]{1,0:T(8,128)(2,1)} %refs_9_.1) | copy-start | bytes 6291460
  32.9 1.6 %copy-start.1 = (bf16[1024,1024]{1,0:T(8,128)(2,1)S(1)}, bf16[1024,1024]{1,0:T(8,128)(2,1)}, u32[]{:S(2)}) copy-start(bf16[1024,1024]{1,0:T(8,128)(2,1)} %refs_7_.3) | copy-start | bytes 6291460
  34.5 13.2 %copy-start.2 = (bf16[1024,1024]{1,0:T(8,128)(2,1)S(1)}, bf16[1024,1024]{1,0:T(8,128)(2,1)}, u32[]{:S(2)}) copy-start(bf16[1024,1024]{1,0:T(8,128)(2,1)} %refs_13_.1) | copy-start | bytes 6291460
  34.5 13.2 %copy-start.4 = (bf16[128,1024]{1,0:T(8,128)(2,1)S(1)}, bf16[128,1024]{1,0:T(8,128)(2,1)}, u32[]{:S(2)}) copy-start(bf16[128,1024]{1,0:T(8,128)(2,1)} %copy-done.3) | copy-start | bytes 786436
  43.7 4.0 %collective-permute-start.13 = (bf16[128,1024]{1,0:T(8,128)(2,1)S(1)}, bf16[128,1024]{1,0:T(8,128)(2,1)S(1)}, u32[]{:S(2)}, u32[]{:S(2)}) collective-permute-start(bf16[128,1024]{1,0:T(8,128)(2,1)S(1)} %collective-permute-done.7.refs_2_), channel_id=1, source_target_pairs={{0,1},{1,0},{2,3},{3,2},{4,5},{5,4},{6,7},{7,6},{8,9},{9,8},{10,11... | collective-permute-start | bytes 786440 | tf_op jit(solution)/shard_map/ppermute | solution.py:45

commit v3 on v2

--- a/solution.py
+++ b/solution.py
@@ -105,7 +105,7 @@
 
 def conv_kernel(
     tok, tile_a, tile_b, halo, halo_a, halo_b, ring_a, ring_b, gains,
-    hidden, second, second_a, second_b, before, middle, after, mixed,
+    hidden, second, second_a, second_b, copy_b, before, middle, after, mixed,
 ):
     rows, cols, width = tok.shape
     gain_one, gain_two = gains[0:1, :], gains[1:2, :]
@@ -168,6 +168,7 @@
             at = slice(row * cols, (row + 1) * cols)
             wide = mixed[at, :].astype(jnp.float32)
             out[at, :] = (wide * unit(wide) * gain_two).astype(jnp.bfloat16)
+    copy_b[...] = second_b[...]
 
 
 def head_marks(model, head):
@@ -222,24 +223,31 @@
     width = 2 * head
     marks = head_marks(model, head)
     if first:
-        raw = jnp.dot(tiles[0][...], w_query[...], preferred_element_type=jnp.float32)
-        queries[...] = head_units(raw, marks, head)
+        raw_query = jnp.dot(tiles[0][...], w_query[...], preferred_element_type=jnp.float32)
     tokens = [ref[...] for ref in tiles]
     if last:
         other = tokens.pop()
         tokens[-1] = jnp.where(band_facts()[3], tokens[-1], other)
     tokens = jnp.concatenate(tokens, axis=0)
-    raw = jnp.dot(tokens, w_key[...], preferred_element_type=jnp.float32)
-    keys[...] = head_units(raw, marks, head)
+    held = None
+    for start in range(0, model, CHUNK):
+        part = slice(start, start + CHUNK)
+        raw = jnp.dot(tokens, w_key[:, part], preferred_element_type=jnp.float32)
+        if held is not None:
+            keys[:, held[0]] = head_units(held[1], marks[:CHUNK], head)
+        elif first:
+            queries[...] = head_units(raw_query, marks, head)
+        held = (part, raw)
     values[...] = lax.dot_general(
         w_value[...], tokens, (((1,), (1,)), ((), ())), preferred_element_type=jnp.float32
     ).astype(jnp.bfloat16)
+    keys[:, held[0]] = head_units(held[1], marks[:CHUNK], head)
 
     flags = slot_penalties(pattern, slots)
     factor = math.log2(math.e) / math.sqrt(head)
     lane = lax.broadcasted_iota(jnp.int32, (size, width), 1)
     half = lax.broadcasted_iota(jnp.int32, (1, 2 * size), 1) < size
-    for pair in range(heads // 2):
+    def weigh(pair):
         lanes = slice(pair * width, (pair + 1) * width)
         query = queries[:, lanes]
         zero = jnp.zeros_like(query)
@@ -260,7 +268,10 @@
         for part in exps[1:]:
             total = total + part
         low = jnp.sum(total, axis=0, keepdims=True)
-        weights = jnp.concatenate([part.astype(jnp.bfloat16) for part in exps], axis=0)
+        return best, low, jnp.concatenate([part.astype(jnp.bfloat16) for part in exps], axis=0)
+
+    def mix(pair, best, low, weights):
+        lanes = slice(pair * width, (pair + 1) * width)
         mixed = jnp.dot(values[lanes, :], weights, preferred_element_type=jnp.float32)
         mixed = jnp.concatenate([mixed[:head, :size], mixed[head:, size:]], axis=0)
         if not first:
@@ -273,6 +284,14 @@
             sums_out[lanes, :] = mixed
             tops_out[pair : pair + 1, :] = best
             lows_out[pair : pair + 1, :] = low
+
+    waiting = []
+    for pair in range(heads // 2):
+        waiting.append((pair, *weigh(pair)))
+        if len(waiting) > 2:
+            mix(*waiting.pop(0))
+    for entry in waiting:
+        mix(*entry)
     if not last:
         return
     attended = joined[...]
@@ -379,11 +398,11 @@
     w_value = jnp.transpose(w_value)
     gains, w_value = lax.optimization_barrier((gains, w_value))
     window = pltpu.VMEM((2 + 3 * rows, cols, model), jnp.float32)
-    hidden, second, second_a, second_b = pl.pallas_call(
+    hidden, second, second_a, second_b, copy_b = pl.pallas_call(
         conv_kernel,
-        out_shape=[tile] * 4,
+        out_shape=[tile] * 5,
         in_specs=[VMEM] * 9,
-        out_specs=[VMEM] * 4,
+        out_specs=[VMEM] * 5,
         scratch_shapes=[window] * 3 + [pltpu.VMEM((size, model), jnp.bfloat16)],
         compiler_params=limit(10),
         cost_estimate=pl.CostEstimate(flops=2**24, bytes_accessed=24 * 2**20, transcendentals=0),
@@ -394,7 +413,7 @@
 
     on = across(second, False)
     off = across(second, True)
-    on_a, on_b = across(second_a, False), across(second_b, False)
+    on_a, on_b = across(second_a, False), across(copy_b, False)
     off_a = across(second_a, True)
     third = across(jnp.where(polar, on, second_b), True)
 

time: 56.1 us -> 54.2 us (0.966)
  Pallas kernels: 21.5 us -> 17.3 us
  waiting for transfers between devices: 10.3 us -> 12.4 us
    pallas_call x2, Pallas kernels: 17.2 us -> 13.1 us  [attend(): pl.pallas_call(functools.partial(group_kernel, heads, slots, first, last)...]
    ppermute x14, waiting for transfers between devices: 10.3 us -> 12.4 us  [permuted(): return lax.ppermute(value, axis, pairs)]
  transfers between devices with their start and end apart: 14 -> 14, of which waited for: 4 -> 5; matrix products, arithmetic and copies ran while one was open for 8% -> 8% of each run, Pallas kernels for 16% -> 13%
where the time goes in v3:
time: 54.2 us; the launch traced here: 53.8 us
  Pallas kernels  17.3 us (32%)
  starting transfers between devices  15.5 us (29%)
  waiting for transfers between devices  12.4 us (23%)
  local copies, waits for them, and re-layouts  7.59 us (14%)
  other arithmetic  0.78 us (1%)
    ppermute x14, starting transfers between devices, permuted(): return lax.ppermute(value, axis, pairs)  15.5 us
    pallas_call x2, Pallas kernels, attend(): pl.pallas_call(functools.partial(group_kernel, heads, slots, first, last)...  13.1 us
    ppermute x14, waiting for transfers between devices, permuted(): return lax.ppermute(value, axis, pairs)  12.4 us
    unnamed x15, local copies, waits for them, and re-layouts  6.76 us
    pallas_call x1, Pallas kernels, on_device(): pl.pallas_call(conv_kernel, out_shape=[tile] * 5, in_specs=[VMEM] * 9, ou...  3.25 us
  transfers between devices with their start and end apart: 14, of which 5 were waited for; matrix products, arithmetic and copies ran while one was open for 8% of the time, Pallas kernels for 13%

profile of v3, /device:TPU:2, one launch (start us, length us, event | category | flops | bytes accessed | tf_op | source)
XLA Modules:
  0.0 53.8 jit_solution(11913390824571506489)
XLA Ops:
  0.0 1.0 %prep.1 = (bf16[8,16,1024]{2,1,0:T(8,128)(2,1)S(1)}, bf16[16,1024]{1,0:T(8,128)(2,1)S(1)}, bf16[32,1024]{1,0:T(8,128)(2,1)S(1)}) custom-call(bf16[8,16,1024]{2,1,0:T(8,128)(2,1)} %tok.1), custom_call_target="tpu_custom_call" | custom-call | bytes 2097152 | tf_op jit(solution)/shard_map/prep/pallas_call | solution.py:368
  1.0 3.1 %collective-permute-start.2 = (bf16[16,1024]{1,0:T(8,128)(2,1)S(1)}, bf16[16,1024]{1,0:T(8,128)(2,1)S(1)}, u32[]{:S(2)}, u32[]{:S(2)}) collective-permute-start(bf16[16,1024]{1,0:T(8,128)(2,1)S(1)} %get-tuple-element.22), channel_id=1, source_target_pairs={{1,2},{2,1},{3,4},{4,3},{5,6},{6,5},{7,0},{0,7},{9,10},{10,9},{11,... | collective-permute-start | bytes 98312 | tf_op jit(solution)/shard_map/ppermute | solution.py:45
  4.1 0.0 collective-permute-start.3
  4.1 0.5 collective-permute-start
  4.7 4.3 %collective-permute-start.1 = (bf16[8,16,1024]{2,1,0:T(8,128)(2,1)}, bf16[8,16,1024]{2,1,0:T(8,128)(2,1)S(1)}, u32[]{:S(2)}, u32[]{:S(2)}) collective-permute-start(bf16[8,16,1024]{2,1,0:T(8,128)(2,1)} %tok.1), channel_id=1, source_target_pairs={{8,16},{16,8},{9,17},{17,9},{10,18},{18,10},{11,19},{19,11},{12,20... | collective-permute-start | bytes 786440 | tf_op jit(solution)/shard_map/ppermute | solution.py:45
  9.0 0.8 %reshape.18 = f32[9,1024]{1,0:T(8,128)S(1)} reshape(f32[3,3,1024]{2,1,0:T(4,128)} %param.12) | data formatting | bytes 73728 | tf_op jit(solution)/shard_map/reshape | solution.py:381
  9.9 0.0 collective-permute-done.2
  9.9 0.0 collective-permute-done.3
  9.9 0.1 collective-permute-start.4
  10.0 2.4 %collective-permute-start.5 = (bf16[16,1024]{1,0:T(8,128)(2,1)S(1)}, bf16[16,1024]{1,0:T(8,128)(2,1)S(1)}, u32[]{:S(2)}, u32[]{:S(2)}) collective-permute-start(bf16[16,1024]{1,0:T(8,128)(2,1)S(1)} %pad_maximum_fusion.2.halo), channel_id=1, source_target_pairs={{8,16},{16,8},{9,17},{17,9},{10,18},{18,10},{11,19},{19,11},{12,20... | collective-permute-start | bytes 98312 | tf_op jit(solution)/shard_map/ppermute | solution.py:45
  12.4 0.1 collective-permute-start.6
  12.5 0.7 %pad_maximum_fusion.1.gains = f32[11,1024]{1,0:T(8,128)S(1)} fusion(f32[9,1024]{1,0:T(8,128)S(1)} %reshape.18, f32[1,1024]{1,0:T(1,128)} %bitcast.9, f32[1,1024]{1,0:T(1,128)} %bitcast.10), kind=kLoop, calls=%fused_computation.2 | loop fusion | flops 22528 | bytes 90112 | tf_op jit(solution)/shard_map/concatenate | solution.py:380
  13.2 0.0 copy-start.5
  13.2 0.0 copy-start.6
  13.2 2.9 %copy.11 = bf16[1024,1024]{0,1:T(8,128)(2,1)S(1)} copy(bf16[1024,1024]{1,0:T(8,128)(2,1)} %param.16) | data formatting | bytes 4194304 | tf_op args[6]
  16.1 1.8 %collective-permute-done.4.halo_a = bf16[16,1024]{1,0:T(8,128)(2,1)S(1)} collective-permute-done((bf16[16,1024]{1,0:T(8,128)(2,1)S(1)}, bf16[16,1024]{1,0:T(8,128)(2,1)S(1)}, u32[]{:S(2)}, u32[]{:S(2)}) %collective-permute-start.4) | collective-permute-done | bytes 32800 | tf_op jit(solution)/shard_map/ppermute | solution.py:45
  17.9 3.3 %collective-permute-done.5.halo_b = bf16[16,1024]{1,0:T(8,128)(2,1)S(1)} collective-permute-done((bf16[16,1024]{1,0:T(8,128)(2,1)S(1)}, bf16[16,1024]{1,0:T(8,128)(2,1)S(1)}, u32[]{:S(2)}, u32[]{:S(2)}) %collective-permute-start.5) | collective-permute-done | bytes 32800 | tf_op jit(solution)/shard_map/ppermute | solution.py:45
  21.1 1.3 %collective-permute-done.6.ring_a = bf16[48,1024]{1,0:T(8,128)(2,1)S(1)} collective-permute-done((bf16[48,1024]{1,0:T(8,128)(2,1)S(1)}, bf16[48,1024]{1,0:T(8,128)(2,1)S(1)}, u32[]{:S(2)}, u32[]{:S(2)}) %collective-permute-start.6) | collective-permute-done | bytes 98336 | tf_op jit(solution)/shard_map/ppermute | solution.py:45
  22.4 0.0 collective-permute-done.tile_a
  22.4 0.0 collective-permute-done.1.tile_b
  22.5 3.3 %conv.1 = (bf16[128,1024]{1,0:T(8,128)(2,1)S(1)}, bf16[128,1024]{1,0:T(8,128)(2,1)}, bf16[128,1024]{1,0:T(8,128)(2,1)}, bf16[128,1024]{1,0:T(8,128)(2,1)S(1)}, bf16[128,1024]{1,0:T(8,128)(2,1)}) custom-call(bf16[8,16,1024]{2,1,0:T(8,128)(2,1)S(1)} %get-tuple-element.21.tok, bf16[8,16,1024]{2,1,0:T(8,128)(2,1)S(1)} %collective-permute-done.tile_a, ...), custom_call_target="tpu_custom_call" | custom-call | flops 16777216 | bytes 25165824 | tf_op jit(solution)/shard_map/conv/pallas_call | solution.py:401
  25.7 0.0 copy-start.3
  25.7 0.7 %copy-done.3 = bf16[128,1024]{1,0:T(8,128)(2,1)} copy-done((bf16[128,1024]{1,0:T(8,128)(2,1)}, bf16[128,1024]{1,0:T(8,128)(2,1)S(1)}, u32[]{:S(2)}) %copy-start.3) | copy-done | bytes 262168
  26.4 0.0 collective-permute-start.8
  26.4 0.5 collective-permute-start.10
  26.9 0.0 collective-permute-start.9
  26.9 0.7 %collective-permute-start.7 = (bf16[128,1024]{1,0:T(8,128)(2,1)}, bf16[128,1024]{1,0:T(8,128)(2,1)S(1)}, u32[]{:S(2)}, u32[]{:S(2)}) collective-permute-start(bf16[128,1024]{1,0:T(8,128)(2,1)} %get-tuple-element.25.refs_2_), channel_id=1, source_target_pairs={{1,2},{2,1},{3,4},{4,3},{5,6},{6,5},{7,0},{0,7},{9,10},{10,9},{11,... | collective-permute-start | bytes 786440 | tf_op jit(solution)/shard_map/ppermute | solution.py:45
  27.7 2.8 %collective-permute-start.11 = (bf16[128,1024]{1,0:T(8,128)(2,1)}, bf16[128,1024]{1,0:T(8,128)(2,1)S(1)}, u32[]{:S(2)}, u32[]{:S(2)}) collective-permute-start(bf16[128,1024]{1,0:T(8,128)(2,1)} %get-tuple-element.26.refs_3_), channel_id=1, source_target_pairs={{1,2},{2,1},{3,4},{4,3},{5,6},{6,5},{7,0},{0,7},{9,10},{10,9},{11,... | collective-permute-start | bytes 786440 | tf_op jit(solution)/shard_map/ppermute | solution.py:45
  30.5 0.0 collective-permute-done.8.refs_4_
  30.5 0.8 %collective-permute-start.12 = (bf16[128,1024]{1,0:T(8,128)(2,1)S(1)}, bf16[128,1024]{1,0:T(8,128)(2,1)S(1)}, u32[]{:S(2)}, u32[]{:S(2)}) collective-permute-start(bf16[128,1024]{1,0:T(8,128)(2,1)S(1)} %broadcast_select_fusion), channel_id=1, source_target_pairs={{1,2},{2,1},{3,4},{4,3},{5,6},{6,5},{7,0},{0,7},{9,10},{10,9},{11,... | collective-permute-start | bytes 786440 | tf_op jit(solution)/shard_map/ppermute | solution.py:45
  31.3 0.0 collective-permute-done.10.refs_6_
  31.3 0.0 collective-permute-done.9.refs_5_
  31.3 0.0 copy-done.5
  31.3 0.0 copy-done.6
  31.3 0.0 copy-start
  31.4 1.6 %copy-done = bf16[1024,1024]{1,0:T(8,128)(2,1)S(1)} copy-done((bf16[1024,1024]{1,0:T(8,128)(2,1)S(1)}, bf16[1024,1024]{1,0:T(8,128)(2,1)}, u32[]{:S(2)}) %copy-start) | copy-done | bytes 2097176
  32.9 0.0 copy-start.1
  32.9 1.6 %copy-done.1 = bf16[1024,1024]{1,0:T(8,128)(2,1)S(1)} copy-done((bf16[1024,1024]{1,0:T(8,128)(2,1)S(1)}, bf16[1024,1024]{1,0:T(8,128)(2,1)}, u32[]{:S(2)}) %copy-start.1) | copy-done | bytes 2097176
  34.5 0.0 copy-start.2
  34.5 7.0 %attend0_1_3_4_5.1 = (bf16[128,1024]{1,0:T(8,128)(2,1)S(1)}, f32[8,256]{1,0:T(8,128)S(1)}, f32[8,256]{1,0:T(8,128)S(1)}, f32[1024,128]{1,0:T(8,128)S(1)}) custom-call(s32[8]{0:T(128)S(1)} %bitcast.7, f32[16]{0:T(128)S(1)} %copy-done.6, bf16[128,1024]{1,0:T(8,128)(2,1)} %get-tuple-element.25.refs_2_, bf16[128,1024]{1,0:T(8,128)(2,1)} %get-tuple-element.26.refs_3_, ...), custom_call_target="tpu_custom_call" | custom-call | flops 68719476736 | bytes 268435456 | tf_op jit(solution)/shard_map/attend0_1_3_4_5/pallas_call | solution.py:336
  41.5 0.0 collective-permute-done.7.refs_2_
  41.6 0.1 collective-permute-start.13
  41.6 1.6 %collective-permute-done.11.refs_3_ = bf16[128,1024]{1,0:T(8,128)(2,1)S(1)} collective-permute-done((bf16[128,1024]{1,0:T(8,128)(2,1)}, bf16[128,1024]{1,0:T(8,128)(2,1)S(1)}, u32[]{:S(2)}, u32[]{:S(2)}) %collective-permute-start.11) | collective-permute-done | bytes 262176 | tf_op jit(solution)/shard_map/ppermute | solution.py:45
  43.2 4.5 %collective-permute-done.12.refs_4_ = bf16[128,1024]{1,0:T(8,128)(2,1)S(1)} collective-permute-done((bf16[128,1024]{1,0:T(8,128)(2,1)S(1)}, bf16[128,1024]{1,0:T(8,128)(2,1)S(1)}, u32[]{:S(2)}, u32[]{:S(2)}) %collective-permute-start.12) | collective-permute-done | bytes 262176 | tf_op jit(solution)/shard_map/ppermute | solution.py:45
  47.7 0.0 collective-permute-done.13.refs_5_
  47.7 0.0 copy-done.2
  47.7 0.0 copy-done.4
  47.7 6.1 %attend6_7_8_9.1 = bf16[128,1024]{1,0:T(8,128)(2,1)} custom-call(s32[8]{0:T(128)S(1)} %bitcast.8, f32[16]{0:T(128)S(1)} %copy-done.6, bf16[128,1024]{1,0:T(8,128)(2,1)S(1)} %collective-permute-done.7.refs_2_, bf16[128,1024]{1,0:T(8,128)(2,1)S(1)} %collective-permute-done.11.refs_3_, bf16[128,1024]{1,0:T(8,128)(2,1)S(1)} %collective-permute-done.12.refs_4_, ...), custom_call_target="tpu_custom_call" | custom-call | flops 68719476736 | bytes 268435456 | tf_op jit(solution)/shard_map/attend6_7_8_9/pallas_call | solution.py:336
  (6 shorter events, 0.1 us)
Async XLA Ops:
  1.0 8.8 %collective-permute-start.2 = (bf16[16,1024]{1,0:T(8,128)(2,1)S(1)}, bf16[16,1024]{1,0:T(8,128)(2,1)S(1)}, u32[]{:S(2)}, u32[]{:S(2)}) collective-permute-start(bf16[16,1024]{1,0:T(8,128)(2,1)S(1)} %get-tuple-element.22), channel_id=1, source_target_pairs={{1,2},{2,1},{3,4},{4,3},{5,6},{6,5},{7,0},{0,7},{9,10},{10,9},{11,... | collective-permute-start | bytes 98312 | tf_op jit(solution)/shard_map/ppermute | solution.py:45
  4.1 5.7 %collective-permute-start.3 = (bf16[16,1024]{1,0:T(8,128)(2,1)S(1)}, bf16[16,1024]{1,0:T(8,128)(2,1)S(1)}, u32[]{:S(2)}, u32[]{:S(2)}) collective-permute-start(bf16[16,1024]{1,0:T(8,128)(2,1)S(1)} %get-tuple-element.22), channel_id=1, source_target_pairs={{0,1},{1,0},{2,3},{3,2},{4,5},{5,4},{6,7},{7,6},{8,9},{9,8},{10,11... | collective-permute-start | bytes 98312 | tf_op jit(solution)/shard_map/ppermute | solution.py:45
  4.1 18.3 %collective-permute-start = (bf16[8,16,1024]{2,1,0:T(8,128)(2,1)}, bf16[8,16,1024]{2,1,0:T(8,128)(2,1)S(1)}, u32[]{:S(2)}, u32[]{:S(2)}) collective-permute-start(bf16[8,16,1024]{2,1,0:T(8,128)(2,1)} %tok.1), channel_id=1, source_target_pairs={{0,8},{8,0},{16,24},{24,16},{1,9},{9,1},{17,25},{25,17},{2,10},{10... | collective-permute-start | bytes 786440 | tf_op jit(solution)/shard_map/ppermute | solution.py:45
  4.7 17.8 %collective-permute-start.1 = (bf16[8,16,1024]{2,1,0:T(8,128)(2,1)}, bf16[8,16,1024]{2,1,0:T(8,128)(2,1)S(1)}, u32[]{:S(2)}, u32[]{:S(2)}) collective-permute-start(bf16[8,16,1024]{2,1,0:T(8,128)(2,1)} %tok.1), channel_id=1, source_target_pairs={{8,16},{16,8},{9,17},{17,9},{10,18},{18,10},{11,19},{19,11},{12,20... | collective-permute-start | bytes 786440 | tf_op jit(solution)/shard_map/ppermute | solution.py:45
  9.9 8.0 %collective-permute-start.4 = (bf16[16,1024]{1,0:T(8,128)(2,1)S(1)}, bf16[16,1024]{1,0:T(8,128)(2,1)S(1)}, u32[]{:S(2)}, u32[]{:S(2)}) collective-permute-start(bf16[16,1024]{1,0:T(8,128)(2,1)S(1)} %pad_maximum_fusion.2.halo), channel_id=1, source_target_pairs={{0,8},{8,0},{16,24},{24,16},{1,9},{9,1},{17,25},{25,17},{2,10},{10... | collective-permute-start | bytes 98312 | tf_op jit(solution)/shard_map/ppermute | solution.py:45
  10.0 11.1 %collective-permute-start.5 = (bf16[16,1024]{1,0:T(8,128)(2,1)S(1)}, bf16[16,1024]{1,0:T(8,128)(2,1)S(1)}, u32[]{:S(2)}, u32[]{:S(2)}) collective-permute-start(bf16[16,1024]{1,0:T(8,128)(2,1)S(1)} %pad_maximum_fusion.2.halo), channel_id=1, source_target_pairs={{8,16},{16,8},{9,17},{17,9},{10,18},{18,10},{11,19},{19,11},{12,20... | collective-permute-start | bytes 98312 | tf_op jit(solution)/shard_map/ppermute | solution.py:45
  12.4 10.0 %collective-permute-start.6 = (bf16[48,1024]{1,0:T(8,128)(2,1)S(1)}, bf16[48,1024]{1,0:T(8,128)(2,1)S(1)}, u32[]{:S(2)}, u32[]{:S(2)}) collective-permute-start(bf16[48,1024]{1,0:T(8,128)(2,1)S(1)} %pad_maximum_fusion), channel_id=1, source_target_pairs={{0,16},{16,0},{8,24},{24,8},{1,17},{17,1},{9,25},{25,9},{2,18},{18... | collective-permute-start | bytes 294920 | tf_op jit(solution)/shard_map/ppermute | solution.py:45
  13.2 18.1 %copy-start.5 = (s32[1,1,8]{2,1,0:T(1,128)S(1)}, s32[1,1,8]{2,1,0:T(1,128)}, u32[]{:S(2)}) copy-start(s32[1,1,8]{2,1,0:T(1,128)} %param.19) | copy-start | bytes 100
  13.2 18.1 %copy-start.6 = (f32[16]{0:T(128)S(1)}, f32[16]{0:T(128)}, u32[]{:S(2)}) copy-start(f32[16]{0:T(128)} %refs_1_.3) | copy-start | bytes 196
  25.7 0.7 %copy-start.3 = (bf16[128,1024]{1,0:T(8,128)(2,1)}, bf16[128,1024]{1,0:T(8,128)(2,1)S(1)}, u32[]{:S(2)}) copy-start(bf16[128,1024]{1,0:T(8,128)(2,1)S(1)} %get-tuple-element.36.refs_14_) | copy-start | bytes 786436
  26.4 4.1 %collective-permute-start.8 = (bf16[128,1024]{1,0:T(8,128)(2,1)}, bf16[128,1024]{1,0:T(8,128)(2,1)S(1)}, u32[]{:S(2)}, u32[]{:S(2)}) collective-permute-start(bf16[128,1024]{1,0:T(8,128)(2,1)} %get-tuple-element.25.refs_2_), channel_id=1, source_target_pairs={{0,1},{1,0},{2,3},{3,2},{4,5},{5,4},{6,7},{7,6},{8,9},{9,8},{10,11... | collective-permute-start | bytes 786440 | tf_op jit(solution)/shard_map/ppermute | solution.py:45
  26.4 4.9 %collective-permute-start.10 = (bf16[128,1024]{1,0:T(8,128)(2,1)}, bf16[128,1024]{1,0:T(8,128)(2,1)S(1)}, u32[]{:S(2)}, u32[]{:S(2)}) collective-permute-start(bf16[128,1024]{1,0:T(8,128)(2,1)} %get-tuple-element.27), channel_id=1, source_target_pairs={{0,1},{1,0},{2,3},{3,2},{4,5},{5,4},{6,7},{7,6},{8,9},{9,8},{10,11... | collective-permute-start | bytes 786440 | tf_op jit(solution)/shard_map/ppermute | solution.py:45
  26.9 4.4 %collective-permute-start.9 = (bf16[128,1024]{1,0:T(8,128)(2,1)}, bf16[128,1024]{1,0:T(8,128)(2,1)S(1)}, u32[]{:S(2)}, u32[]{:S(2)}) collective-permute-start(bf16[128,1024]{1,0:T(8,128)(2,1)} %get-tuple-element.26.refs_3_), channel_id=1, source_target_pairs={{0,1},{1,0},{2,3},{3,2},{4,5},{5,4},{6,7},{7,6},{8,9},{9,8},{10,11... | collective-permute-start | bytes 786440 | tf_op jit(solution)/shard_map/ppermute | solution.py:45
  26.9 14.6 %collective-permute-start.7 = (bf16[128,1024]{1,0:T(8,128)(2,1)}, bf16[128,1024]{1,0:T(8,128)(2,1)S(1)}, u32[]{:S(2)}, u32[]{:S(2)}) collective-permute-start(bf16[128,1024]{1,0:T(8,128)(2,1)} %get-tuple-element.25.refs_2_), channel_id=1, source_target_pairs={{1,2},{2,1},{3,4},{4,3},{5,6},{6,5},{7,0},{0,7},{9,10},{10,9},{11,... | collective-permute-start | bytes 786440 | tf_op jit(solution)/shard_map/ppermute | solution.py:45
  27.7 15.5 %collective-permute-start.11 = (bf16[128,1024]{1,0:T(8,128)(2,1)}, bf16[128,1024]{1,0:T(8,128)(2,1)S(1)}, u32[]{:S(2)}, u32[]{:S(2)}) collective-permute-start(bf16[128,1024]{1,0:T(8,128)(2,1)} %get-tuple-element.26.refs_3_), channel_id=1, source_target_pairs={{1,2},{2,1},{3,4},{4,3},{5,6},{6,5},{7,0},{0,7},{9,10},{10,9},{11,... | collective-permute-start | bytes 786440 | tf_op jit(solution)/shard_map/ppermute | solution.py:45
  30.5 17.2 %collective-permute-start.12 = (bf16[128,1024]{1,0:T(8,128)(2,1)S(1)}, bf16[128,1024]{1,0:T(8,128)(2,1)S(1)}, u32[]{:S(2)}, u32[]{:S(2)}) collective-permute-start(bf16[128,1024]{1,0:T(8,128)(2,1)S(1)} %broadcast_select_fusion), channel_id=1, source_target_pairs={{1,2},{2,1},{3,4},{4,3},{5,6},{6,5},{7,0},{0,7},{9,10},{10,9},{11,... | collective-permute-start | bytes 786440 | tf_op jit(solution)/shard_map/ppermute | solution.py:45
  31.3 1.6 %copy-start = (bf16[1024,1024]{1,0:T(8,128)(2,1)S(1)}, bf16[1024,1024]{1,0:T(8,128)(2,1)}, u32[]{:S(2)}) copy-start(bf16[1024,1024]{1,0:T(8,128)(2,1)} %refs_9_.1) | copy-start | bytes 6291460
  32.9 1.6 %copy-start.1 = (bf16[1024,1024]{1,0:T(8,128)(2,1)S(1)}, bf16[1024,1024]{1,0:T(8,128)(2,1)}, u32[]{:S(2)}) copy-start(bf16[1024,1024]{1,0:T(8,128)(2,1)} %refs_7_.3) | copy-start | bytes 6291460
  34.5 13.2 %copy-start.2 = (bf16[1024,1024]{1,0:T(8,128)(2,1)S(1)}, bf16[1024,1024]{1,0:T(8,128)(2,1)}, u32[]{:S(2)}) copy-start(bf16[1024,1024]{1,0:T(8,128)(2,1)} %refs_13_.1) | copy-start | bytes 6291460
  34.5 13.2 %copy-start.4 = (bf16[128,1024]{1,0:T(8,128)(2,1)S(1)}, bf16[128,1024]{1,0:T(8,128)(2,1)}, u32[]{:S(2)}) copy-start(bf16[128,1024]{1,0:T(8,128)(2,1)} %copy-done.3) | copy-start | bytes 786436
  41.6 6.2 %collective-permute-start.13 = (bf16[128,1024]{1,0:T(8,128)(2,1)S(1)}, bf16[128,1024]{1,0:T(8,128)(2,1)S(1)}, u32[]{:S(2)}, u32[]{:S(2)}) collective-permute-start(bf16[128,1024]{1,0:T(8,128)(2,1)S(1)} %collective-permute-done.7.refs_2_), channel_id=1, source_target_pairs={{0,1},{1,0},{2,3},{3,2},{4,5},{5,4},{6,7},{7,6},{8,9},{9,8},{10,11... | collective-permute-start | bytes 786440 | tf_op jit(solution)/shard_map/ppermute | solution.py:45

commit v4 on v3

--- a/solution.py
+++ b/solution.py
@@ -288,7 +288,7 @@
     waiting = []
     for pair in range(heads // 2):
         waiting.append((pair, *weigh(pair)))
-        if len(waiting) > 2:
+        if len(waiting) > 3:
             mix(*waiting.pop(0))
     for entry in waiting:
         mix(*entry)

time: 54.2 us -> 54.1 us (level)
  no operation moved by 1% of the time
where the time goes in v4:
time: 54.1 us; the launch traced here: 53.7 us
  Pallas kernels  17.4 us (32%)
  starting transfers between devices  15.5 us (29%)
  waiting for transfers between devices  12.4 us (23%)
  local copies, waits for them, and re-layouts  7.59 us (14%)
  other arithmetic  0.78 us (1%)
    ppermute x14, starting transfers between devices, permuted(): return lax.ppermute(value, axis, pairs)  15.5 us
    pallas_call x2, Pallas kernels, attend(): pl.pallas_call(functools.partial(group_kernel, heads, slots, first, last)...  13.1 us
    ppermute x14, waiting for transfers between devices, permuted(): return lax.ppermute(value, axis, pairs)  12.4 us
    unnamed x15, local copies, waits for them, and re-layouts  6.76 us
    pallas_call x1, Pallas kernels, on_device(): pl.pallas_call(conv_kernel, out_shape=[tile] * 5, in_specs=[VMEM] * 9, ou...  3.25 us
  transfers between devices with their start and end apart: 14, of which 5 were waited for; matrix products, arithmetic and copies ran while one was open for 8% of the time, Pallas kernels for 13%

profile of v4, /device:TPU:2, one launch (start us, length us, event | category | flops | bytes accessed | tf_op | source)
XLA Modules:
  0.0 53.7 jit_solution(1776011175443183434)
XLA Ops:
  0.0 1.0 %prep.1 = (bf16[8,16,1024]{2,1,0:T(8,128)(2,1)S(1)}, bf16[16,1024]{1,0:T(8,128)(2,1)S(1)}, bf16[32,1024]{1,0:T(8,128)(2,1)S(1)}) custom-call(bf16[8,16,1024]{2,1,0:T(8,128)(2,1)} %tok.1), custom_call_target="tpu_custom_call" | custom-call | bytes 2097152 | tf_op jit(solution)/shard_map/prep/pallas_call | solution.py:368
  1.0 3.1 %collective-permute-start.2 = (bf16[16,1024]{1,0:T(8,128)(2,1)S(1)}, bf16[16,1024]{1,0:T(8,128)(2,1)S(1)}, u32[]{:S(2)}, u32[]{:S(2)}) collective-permute-start(bf16[16,1024]{1,0:T(8,128)(2,1)S(1)} %get-tuple-element.22), channel_id=1, source_target_pairs={{1,2},{2,1},{3,4},{4,3},{5,6},{6,5},{7,0},{0,7},{9,10},{10,9},{11,... | collective-permute-start | bytes 98312 | tf_op jit(solution)/shard_map/ppermute | solution.py:45
  4.1 0.0 collective-permute-start.3
  4.1 0.5 collective-permute-start
  4.7 4.3 %collective-permute-start.1 = (bf16[8,16,1024]{2,1,0:T(8,128)(2,1)}, bf16[8,16,1024]{2,1,0:T(8,128)(2,1)S(1)}, u32[]{:S(2)}, u32[]{:S(2)}) collective-permute-start(bf16[8,16,1024]{2,1,0:T(8,128)(2,1)} %tok.1), channel_id=1, source_target_pairs={{8,16},{16,8},{9,17},{17,9},{10,18},{18,10},{11,19},{19,11},{12,20... | collective-permute-start | bytes 786440 | tf_op jit(solution)/shard_map/ppermute | solution.py:45
  9.0 0.8 %reshape.18 = f32[9,1024]{1,0:T(8,128)S(1)} reshape(f32[3,3,1024]{2,1,0:T(4,128)} %param.12) | data formatting | bytes 73728 | tf_op jit(solution)/shard_map/reshape | solution.py:381
  9.9 0.0 collective-permute-done.2
  9.9 0.0 collective-permute-done.3
  9.9 0.1 collective-permute-start.4
  10.0 2.4 %collective-permute-start.5 = (bf16[16,1024]{1,0:T(8,128)(2,1)S(1)}, bf16[16,1024]{1,0:T(8,128)(2,1)S(1)}, u32[]{:S(2)}, u32[]{:S(2)}) collective-permute-start(bf16[16,1024]{1,0:T(8,128)(2,1)S(1)} %pad_maximum_fusion.2.halo), channel_id=1, source_target_pairs={{8,16},{16,8},{9,17},{17,9},{10,18},{18,10},{11,19},{19,11},{12,20... | collective-permute-start | bytes 98312 | tf_op jit(solution)/shard_map/ppermute | solution.py:45
  12.4 0.1 collective-permute-start.6
  12.5 0.7 %pad_maximum_fusion.1.gains = f32[11,1024]{1,0:T(8,128)S(1)} fusion(f32[9,1024]{1,0:T(8,128)S(1)} %reshape.18, f32[1,1024]{1,0:T(1,128)} %bitcast.9, f32[1,1024]{1,0:T(1,128)} %bitcast.10), kind=kLoop, calls=%fused_computation.2 | loop fusion | flops 22528 | bytes 90112 | tf_op jit(solution)/shard_map/concatenate | solution.py:380
  13.2 0.0 copy-start.5
  13.2 0.0 copy-start.6
  13.2 2.9 %copy.11 = bf16[1024,1024]{0,1:T(8,128)(2,1)S(1)} copy(bf16[1024,1024]{1,0:T(8,128)(2,1)} %param.16) | data formatting | bytes 4194304 | tf_op args[6]
  16.1 1.8 %collective-permute-done.4.halo_a = bf16[16,1024]{1,0:T(8,128)(2,1)S(1)} collective-permute-done((bf16[16,1024]{1,0:T(8,128)(2,1)S(1)}, bf16[16,1024]{1,0:T(8,128)(2,1)S(1)}, u32[]{:S(2)}, u32[]{:S(2)}) %collective-permute-start.4) | collective-permute-done | bytes 32800 | tf_op jit(solution)/shard_map/ppermute | solution.py:45
  17.9 3.3 %collective-permute-done.5.halo_b = bf16[16,1024]{1,0:T(8,128)(2,1)S(1)} collective-permute-done((bf16[16,1024]{1,0:T(8,128)(2,1)S(1)}, bf16[16,1024]{1,0:T(8,128)(2,1)S(1)}, u32[]{:S(2)}, u32[]{:S(2)}) %collective-permute-start.5) | collective-permute-done | bytes 32800 | tf_op jit(solution)/shard_map/ppermute | solution.py:45
  21.1 1.3 %collective-permute-done.6.ring_a = bf16[48,1024]{1,0:T(8,128)(2,1)S(1)} collective-permute-done((bf16[48,1024]{1,0:T(8,128)(2,1)S(1)}, bf16[48,1024]{1,0:T(8,128)(2,1)S(1)}, u32[]{:S(2)}, u32[]{:S(2)}) %collective-permute-start.6) | collective-permute-done | bytes 98336 | tf_op jit(solution)/shard_map/ppermute | solution.py:45
  22.4 0.0 collective-permute-done.tile_a
  22.4 0.0 collective-permute-done.1.tile_b
  22.5 3.3 %conv.1 = (bf16[128,1024]{1,0:T(8,128)(2,1)S(1)}, bf16[128,1024]{1,0:T(8,128)(2,1)}, bf16[128,1024]{1,0:T(8,128)(2,1)}, bf16[128,1024]{1,0:T(8,128)(2,1)S(1)}, bf16[128,1024]{1,0:T(8,128)(2,1)}) custom-call(bf16[8,16,1024]{2,1,0:T(8,128)(2,1)S(1)} %get-tuple-element.21.tok, bf16[8,16,1024]{2,1,0:T(8,128)(2,1)S(1)} %collective-permute-done.tile_a, ...), custom_call_target="tpu_custom_call" | custom-call | flops 16777216 | bytes 25165824 | tf_op jit(solution)/shard_map/conv/pallas_call | solution.py:401
  25.7 0.0 copy-start.3
  25.7 0.7 %copy-done.3 = bf16[128,1024]{1,0:T(8,128)(2,1)} copy-done((bf16[128,1024]{1,0:T(8,128)(2,1)}, bf16[128,1024]{1,0:T(8,128)(2,1)S(1)}, u32[]{:S(2)}) %copy-start.3) | copy-done | bytes 262168
  26.4 0.0 collective-permute-start.8
  26.4 0.5 collective-permute-start.10
  26.9 0.0 collective-permute-start.9
  26.9 0.7 %collective-permute-start.7 = (bf16[128,1024]{1,0:T(8,128)(2,1)}, bf16[128,1024]{1,0:T(8,128)(2,1)S(1)}, u32[]{:S(2)}, u32[]{:S(2)}) collective-permute-start(bf16[128,1024]{1,0:T(8,128)(2,1)} %get-tuple-element.25.refs_2_), channel_id=1, source_target_pairs={{1,2},{2,1},{3,4},{4,3},{5,6},{6,5},{7,0},{0,7},{9,10},{10,9},{11,... | collective-permute-start | bytes 786440 | tf_op jit(solution)/shard_map/ppermute | solution.py:45
  27.7 2.8 %collective-permute-start.11 = (bf16[128,1024]{1,0:T(8,128)(2,1)}, bf16[128,1024]{1,0:T(8,128)(2,1)S(1)}, u32[]{:S(2)}, u32[]{:S(2)}) collective-permute-start(bf16[128,1024]{1,0:T(8,128)(2,1)} %get-tuple-element.26.refs_3_), channel_id=1, source_target_pairs={{1,2},{2,1},{3,4},{4,3},{5,6},{6,5},{7,0},{0,7},{9,10},{10,9},{11,... | collective-permute-start | bytes 786440 | tf_op jit(solution)/shard_map/ppermute | solution.py:45
  30.5 0.0 collective-permute-done.8.refs_4_
  30.5 0.8 %collective-permute-start.12 = (bf16[128,1024]{1,0:T(8,128)(2,1)S(1)}, bf16[128,1024]{1,0:T(8,128)(2,1)S(1)}, u32[]{:S(2)}, u32[]{:S(2)}) collective-permute-start(bf16[128,1024]{1,0:T(8,128)(2,1)S(1)} %broadcast_select_fusion), channel_id=1, source_target_pairs={{1,2},{2,1},{3,4},{4,3},{5,6},{6,5},{7,0},{0,7},{9,10},{10,9},{11,... | collective-permute-start | bytes 786440 | tf_op jit(solution)/shard_map/ppermute | solution.py:45
  31.3 0.0 collective-permute-done.10.refs_6_
  31.3 0.0 collective-permute-done.9.refs_5_
  31.3 0.0 copy-done.5
  31.3 0.0 copy-done.6
  31.3 0.0 copy-start
  31.4 1.6 %copy-done = bf16[1024,1024]{1,0:T(8,128)(2,1)S(1)} copy-done((bf16[1024,1024]{1,0:T(8,128)(2,1)S(1)}, bf16[1024,1024]{1,0:T(8,128)(2,1)}, u32[]{:S(2)}) %copy-start) | copy-done | bytes 2097176
  32.9 0.0 copy-start.1
  32.9 1.6 %copy-done.1 = bf16[1024,1024]{1,0:T(8,128)(2,1)S(1)} copy-done((bf16[1024,1024]{1,0:T(8,128)(2,1)S(1)}, bf16[1024,1024]{1,0:T(8,128)(2,1)}, u32[]{:S(2)}) %copy-start.1) | copy-done | bytes 2097176
  34.5 0.0 copy-start.2
  34.5 7.1 %attend0_1_3_4_5.1 = (bf16[128,1024]{1,0:T(8,128)(2,1)S(1)}, f32[8,256]{1,0:T(8,128)S(1)}, f32[8,256]{1,0:T(8,128)S(1)}, f32[1024,128]{1,0:T(8,128)S(1)}) custom-call(s32[8]{0:T(128)S(1)} %bitcast.7, f32[16]{0:T(128)S(1)} %copy-done.6, bf16[128,1024]{1,0:T(8,128)(2,1)} %get-tuple-element.25.refs_2_, bf16[128,1024]{1,0:T(8,128)(2,1)} %get-tuple-element.26.refs_3_, ...), custom_call_target="tpu_custom_call" | custom-call | flops 68719476736 | bytes 268435456 | tf_op jit(solution)/shard_map/attend0_1_3_4_5/pallas_call | solution.py:336
  41.6 0.0 collective-permute-done.7.refs_2_
  41.6 0.1 collective-permute-start.13
  41.7 1.5 %collective-permute-done.11.refs_3_ = bf16[128,1024]{1,0:T(8,128)(2,1)S(1)} collective-permute-done((bf16[128,1024]{1,0:T(8,128)(2,1)}, bf16[128,1024]{1,0:T(8,128)(2,1)S(1)}, u32[]{:S(2)}, u32[]{:S(2)}) %collective-permute-start.11) | collective-permute-done | bytes 262176 | tf_op jit(solution)/shard_map/ppermute | solution.py:45
  43.2 4.5 %collective-permute-done.12.refs_4_ = bf16[128,1024]{1,0:T(8,128)(2,1)S(1)} collective-permute-done((bf16[128,1024]{1,0:T(8,128)(2,1)S(1)}, bf16[128,1024]{1,0:T(8,128)(2,1)S(1)}, u32[]{:S(2)}, u32[]{:S(2)}) %collective-permute-start.12) | collective-permute-done | bytes 262176 | tf_op jit(solution)/shard_map/ppermute | solution.py:45
  47.7 0.0 collective-permute-done.13.refs_5_
  47.7 0.0 copy-done.2
  47.7 0.0 copy-done.4
  47.7 6.0 %attend6_7_8_9.1 = bf16[128,1024]{1,0:T(8,128)(2,1)} custom-call(s32[8]{0:T(128)S(1)} %bitcast.8, f32[16]{0:T(128)S(1)} %copy-done.6, bf16[128,1024]{1,0:T(8,128)(2,1)S(1)} %collective-permute-done.7.refs_2_, bf16[128,1024]{1,0:T(8,128)(2,1)S(1)} %collective-permute-done.11.refs_3_, bf16[128,1024]{1,0:T(8,128)(2,1)S(1)} %collective-permute-done.12.refs_4_, ...), custom_call_target="tpu_custom_call" | custom-call | flops 68719476736 | bytes 268435456 | tf_op jit(solution)/shard_map/attend6_7_8_9/pallas_call | solution.py:336
  (6 shorter events, 0.1 us)
Async XLA Ops:
  1.0 8.8 %collective-permute-start.2 = (bf16[16,1024]{1,0:T(8,128)(2,1)S(1)}, bf16[16,1024]{1,0:T(8,128)(2,1)S(1)}, u32[]{:S(2)}, u32[]{:S(2)}) collective-permute-start(bf16[16,1024]{1,0:T(8,128)(2,1)S(1)} %get-tuple-element.22), channel_id=1, source_target_pairs={{1,2},{2,1},{3,4},{4,3},{5,6},{6,5},{7,0},{0,7},{9,10},{10,9},{11,... | collective-permute-start | bytes 98312 | tf_op jit(solution)/shard_map/ppermute | solution.py:45
  4.1 5.7 %collective-permute-start.3 = (bf16[16,1024]{1,0:T(8,128)(2,1)S(1)}, bf16[16,1024]{1,0:T(8,128)(2,1)S(1)}, u32[]{:S(2)}, u32[]{:S(2)}) collective-permute-start(bf16[16,1024]{1,0:T(8,128)(2,1)S(1)} %get-tuple-element.22), channel_id=1, source_target_pairs={{0,1},{1,0},{2,3},{3,2},{4,5},{5,4},{6,7},{7,6},{8,9},{9,8},{10,11... | collective-permute-start | bytes 98312 | tf_op jit(solution)/shard_map/ppermute | solution.py:45
  4.1 18.3 %collective-permute-start = (bf16[8,16,1024]{2,1,0:T(8,128)(2,1)}, bf16[8,16,1024]{2,1,0:T(8,128)(2,1)S(1)}, u32[]{:S(2)}, u32[]{:S(2)}) collective-permute-start(bf16[8,16,1024]{2,1,0:T(8,128)(2,1)} %tok.1), channel_id=1, source_target_pairs={{0,8},{8,0},{16,24},{24,16},{1,9},{9,1},{17,25},{25,17},{2,10},{10... | collective-permute-start | bytes 786440 | tf_op jit(solution)/shard_map/ppermute | solution.py:45
  4.7 17.8 %collective-permute-start.1 = (bf16[8,16,1024]{2,1,0:T(8,128)(2,1)}, bf16[8,16,1024]{2,1,0:T(8,128)(2,1)S(1)}, u32[]{:S(2)}, u32[]{:S(2)}) collective-permute-start(bf16[8,16,1024]{2,1,0:T(8,128)(2,1)} %tok.1), channel_id=1, source_target_pairs={{8,16},{16,8},{9,17},{17,9},{10,18},{18,10},{11,19},{19,11},{12,20... | collective-permute-start | bytes 786440 | tf_op jit(solution)/shard_map/ppermute | solution.py:45
  9.9 8.0 %collective-permute-start.4 = (bf16[16,1024]{1,0:T(8,128)(2,1)S(1)}, bf16[16,1024]{1,0:T(8,128)(2,1)S(1)}, u32[]{:S(2)}, u32[]{:S(2)}) collective-permute-start(bf16[16,1024]{1,0:T(8,128)(2,1)S(1)} %pad_maximum_fusion.2.halo), channel_id=1, source_target_pairs={{0,8},{8,0},{16,24},{24,16},{1,9},{9,1},{17,25},{25,17},{2,10},{10... | collective-permute-start | bytes 98312 | tf_op jit(solution)/shard_map/ppermute | solution.py:45
  10.0 11.1 %collective-permute-start.5 = (bf16[16,1024]{1,0:T(8,128)(2,1)S(1)}, bf16[16,1024]{1,0:T(8,128)(2,1)S(1)}, u32[]{:S(2)}, u32[]{:S(2)}) collective-permute-start(bf16[16,1024]{1,0:T(8,128)(2,1)S(1)} %pad_maximum_fusion.2.halo), channel_id=1, source_target_pairs={{8,16},{16,8},{9,17},{17,9},{10,18},{18,10},{11,19},{19,11},{12,20... | collective-permute-start | bytes 98312 | tf_op jit(solution)/shard_map/ppermute | solution.py:45
  12.4 10.0 %collective-permute-start.6 = (bf16[48,1024]{1,0:T(8,128)(2,1)S(1)}, bf16[48,1024]{1,0:T(8,128)(2,1)S(1)}, u32[]{:S(2)}, u32[]{:S(2)}) collective-permute-start(bf16[48,1024]{1,0:T(8,128)(2,1)S(1)} %pad_maximum_fusion), channel_id=1, source_target_pairs={{0,16},{16,0},{8,24},{24,8},{1,17},{17,1},{9,25},{25,9},{2,18},{18... | collective-permute-start | bytes 294920 | tf_op jit(solution)/shard_map/ppermute | solution.py:45
  13.2 18.1 %copy-start.5 = (s32[1,1,8]{2,1,0:T(1,128)S(1)}, s32[1,1,8]{2,1,0:T(1,128)}, u32[]{:S(2)}) copy-start(s32[1,1,8]{2,1,0:T(1,128)} %param.19) | copy-start | bytes 100
  13.2 18.1 %copy-start.6 = (f32[16]{0:T(128)S(1)}, f32[16]{0:T(128)}, u32[]{:S(2)}) copy-start(f32[16]{0:T(128)} %refs_1_.3) | copy-start | bytes 196
  25.7 0.7 %copy-start.3 = (bf16[128,1024]{1,0:T(8,128)(2,1)}, bf16[128,1024]{1,0:T(8,128)(2,1)S(1)}, u32[]{:S(2)}) copy-start(bf16[128,1024]{1,0:T(8,128)(2,1)S(1)} %get-tuple-element.36.refs_14_) | copy-start | bytes 786436
  26.4 4.1 %collective-permute-start.8 = (bf16[128,1024]{1,0:T(8,128)(2,1)}, bf16[128,1024]{1,0:T(8,128)(2,1)S(1)}, u32[]{:S(2)}, u32[]{:S(2)}) collective-permute-start(bf16[128,1024]{1,0:T(8,128)(2,1)} %get-tuple-element.25.refs_2_), channel_id=1, source_target_pairs={{0,1},{1,0},{2,3},{3,2},{4,5},{5,4},{6,7},{7,6},{8,9},{9,8},{10,11... | collective-permute-start | bytes 786440 | tf_op jit(solution)/shard_map/ppermute | solution.py:45
  26.4 4.9 %collective-permute-start.10 = (bf16[128,1024]{1,0:T(8,128)(2,1)}, bf16[128,1024]{1,0:T(8,128)(2,1)S(1)}, u32[]{:S(2)}, u32[]{:S(2)}) collective-permute-start(bf16[128,1024]{1,0:T(8,128)(2,1)} %get-tuple-element.27), channel_id=1, source_target_pairs={{0,1},{1,0},{2,3},{3,2},{4,5},{5,4},{6,7},{7,6},{8,9},{9,8},{10,11... | collective-permute-start | bytes 786440 | tf_op jit(solution)/shard_map/ppermute | solution.py:45
  26.9 4.4 %collective-permute-start.9 = (bf16[128,1024]{1,0:T(8,128)(2,1)}, bf16[128,1024]{1,0:T(8,128)(2,1)S(1)}, u32[]{:S(2)}, u32[]{:S(2)}) collective-permute-start(bf16[128,1024]{1,0:T(8,128)(2,1)} %get-tuple-element.26.refs_3_), channel_id=1, source_target_pairs={{0,1},{1,0},{2,3},{3,2},{4,5},{5,4},{6,7},{7,6},{8,9},{9,8},{10,11... | collective-permute-start | bytes 786440 | tf_op jit(solution)/shard_map/ppermute | solution.py:45
  26.9 14.7 %collective-permute-start.7 = (bf16[128,1024]{1,0:T(8,128)(2,1)}, bf16[128,1024]{1,0:T(8,128)(2,1)S(1)}, u32[]{:S(2)}, u32[]{:S(2)}) collective-permute-start(bf16[128,1024]{1,0:T(8,128)(2,1)} %get-tuple-element.25.refs_2_), channel_id=1, source_target_pairs={{1,2},{2,1},{3,4},{4,3},{5,6},{6,5},{7,0},{0,7},{9,10},{10,9},{11,... | collective-permute-start | bytes 786440 | tf_op jit(solution)/shard_map/ppermute | solution.py:45
  27.7 15.5 %collective-permute-start.11 = (bf16[128,1024]{1,0:T(8,128)(2,1)}, bf16[128,1024]{1,0:T(8,128)(2,1)S(1)}, u32[]{:S(2)}, u32[]{:S(2)}) collective-permute-start(bf16[128,1024]{1,0:T(8,128)(2,1)} %get-tuple-element.26.refs_3_), channel_id=1, source_target_pairs={{1,2},{2,1},{3,4},{4,3},{5,6},{6,5},{7,0},{0,7},{9,10},{10,9},{11,... | collective-permute-start | bytes 786440 | tf_op jit(solution)/shard_map/ppermute | solution.py:45
  30.5 17.2 %collective-permute-start.12 = (bf16[128,1024]{1,0:T(8,128)(2,1)S(1)}, bf16[128,1024]{1,0:T(8,128)(2,1)S(1)}, u32[]{:S(2)}, u32[]{:S(2)}) collective-permute-start(bf16[128,1024]{1,0:T(8,128)(2,1)S(1)} %broadcast_select_fusion), channel_id=1, source_target_pairs={{1,2},{2,1},{3,4},{4,3},{5,6},{6,5},{7,0},{0,7},{9,10},{10,9},{11,... | collective-permute-start | bytes 786440 | tf_op jit(solution)/shard_map/ppermute | solution.py:45
  31.3 1.6 %copy-start = (bf16[1024,1024]{1,0:T(8,128)(2,1)S(1)}, bf16[1024,1024]{1,0:T(8,128)(2,1)}, u32[]{:S(2)}) copy-start(bf16[1024,1024]{1,0:T(8,128)(2,1)} %refs_9_.1) | copy-start | bytes 6291460
  32.9 1.6 %copy-start.1 = (bf16[1024,1024]{1,0:T(8,128)(2,1)S(1)}, bf16[1024,1024]{1,0:T(8,128)(2,1)}, u32[]{:S(2)}) copy-start(bf16[1024,1024]{1,0:T(8,128)(2,1)} %refs_7_.3) | copy-start | bytes 6291460
  34.5 13.2 %copy-start.2 = (bf16[1024,1024]{1,0:T(8,128)(2,1)S(1)}, bf16[1024,1024]{1,0:T(8,128)(2,1)}, u32[]{:S(2)}) copy-start(bf16[1024,1024]{1,0:T(8,128)(2,1)} %refs_13_.1) | copy-start | bytes 6291460
  34.5 13.2 %copy-start.4 = (bf16[128,1024]{1,0:T(8,128)(2,1)S(1)}, bf16[128,1024]{1,0:T(8,128)(2,1)}, u32[]{:S(2)}) copy-start(bf16[128,1024]{1,0:T(8,128)(2,1)} %copy-done.3) | copy-start | bytes 786436
  41.6 6.1 %collective-permute-start.13 = (bf16[128,1024]{1,0:T(8,128)(2,1)S(1)}, bf16[128,1024]{1,0:T(8,128)(2,1)S(1)}, u32[]{:S(2)}, u32[]{:S(2)}) collective-permute-start(bf16[128,1024]{1,0:T(8,128)(2,1)S(1)} %collective-permute-done.7.refs_2_), channel_id=1, source_target_pairs={{0,1},{1,0},{2,3},{3,2},{4,5},{5,4},{6,7},{7,6},{8,9},{9,8},{10,11... | collective-permute-start | bytes 786440 | tf_op jit(solution)/shard_map/ppermute | solution.py:45

commit v5 on v4

--- a/solution.py
+++ b/solution.py
@@ -288,7 +288,7 @@
     waiting = []
     for pair in range(heads // 2):
         waiting.append((pair, *weigh(pair)))
-        if len(waiting) > 3:
+        if len(waiting) > 4:
             mix(*waiting.pop(0))
     for entry in waiting:
         mix(*entry)

time: 54.1 us -> 54.2 us (level)
  no operation moved by 1% of the time
where the time goes in v5:
time: 54.2 us; the launch traced here: 53.8 us
  Pallas kernels  17.3 us (32%)
  starting transfers between devices  15.5 us (29%)
  waiting for transfers between devices  12.4 us (23%)
  local copies, waits for them, and re-layouts  7.59 us (14%)
  other arithmetic  0.78 us (1%)
    ppermute x14, starting transfers between devices, permuted(): return lax.ppermute(value, axis, pairs)  15.5 us
    pallas_call x2, Pallas kernels, attend(): pl.pallas_call(functools.partial(group_kernel, heads, slots, first, last)...  13 us
    ppermute x14, waiting for transfers between devices, permuted(): return lax.ppermute(value, axis, pairs)  12.4 us
    unnamed x15, local copies, waits for them, and re-layouts  6.76 us
    pallas_call x1, Pallas kernels, on_device(): pl.pallas_call(conv_kernel, out_shape=[tile] * 5, in_specs=[VMEM] * 9, ou...  3.25 us
  transfers between devices with their start and end apart: 14, of which 5 were waited for; matrix products, arithmetic and copies ran while one was open for 8% of the time, Pallas kernels for 13%

profile of v5, /device:TPU:2, one launch (start us, length us, event | category | flops | bytes accessed | tf_op | source)
XLA Modules:
  0.0 53.8 jit_solution(14799214883386939194)
XLA Ops:
  0.0 1.0 %prep.1 = (bf16[8,16,1024]{2,1,0:T(8,128)(2,1)S(1)}, bf16[16,1024]{1,0:T(8,128)(2,1)S(1)}, bf16[32,1024]{1,0:T(8,128)(2,1)S(1)}) custom-call(bf16[8,16,1024]{2,1,0:T(8,128)(2,1)} %tok.1), custom_call_target="tpu_custom_call" | custom-call | bytes 2097152 | tf_op jit(solution)/shard_map/prep/pallas_call | solution.py:368
  1.0 3.1 %collective-permute-start.2 = (bf16[16,1024]{1,0:T(8,128)(2,1)S(1)}, bf16[16,1024]{1,0:T(8,128)(2,1)S(1)}, u32[]{:S(2)}, u32[]{:S(2)}) collective-permute-start(bf16[16,1024]{1,0:T(8,128)(2,1)S(1)} %get-tuple-element.22), channel_id=1, source_target_pairs={{1,2},{2,1},{3,4},{4,3},{5,6},{6,5},{7,0},{0,7},{9,10},{10,9},{11,... | collective-permute-start | bytes 98312 | tf_op jit(solution)/shard_map/ppermute | solution.py:45
  4.1 0.0 collective-permute-start.3
  4.1 0.5 collective-permute-start
  4.7 4.3 %collective-permute-start.1 = (bf16[8,16,1024]{2,1,0:T(8,128)(2,1)}, bf16[8,16,1024]{2,1,0:T(8,128)(2,1)S(1)}, u32[]{:S(2)}, u32[]{:S(2)}) collective-permute-start(bf16[8,16,1024]{2,1,0:T(8,128)(2,1)} %tok.1), channel_id=1, source_target_pairs={{8,16},{16,8},{9,17},{17,9},{10,18},{18,10},{11,19},{19,11},{12,20... | collective-permute-start | bytes 786440 | tf_op jit(solution)/shard_map/ppermute | solution.py:45
  9.0 0.8 %reshape.18 = f32[9,1024]{1,0:T(8,128)S(1)} reshape(f32[3,3,1024]{2,1,0:T(4,128)} %param.12) | data formatting | bytes 73728 | tf_op jit(solution)/shard_map/reshape | solution.py:381
  9.9 0.0 collective-permute-done.2
  9.9 0.0 collective-permute-done.3
  9.9 0.1 collective-permute-start.4
  10.0 2.4 %collective-permute-start.5 = (bf16[16,1024]{1,0:T(8,128)(2,1)S(1)}, bf16[16,1024]{1,0:T(8,128)(2,1)S(1)}, u32[]{:S(2)}, u32[]{:S(2)}) collective-permute-start(bf16[16,1024]{1,0:T(8,128)(2,1)S(1)} %pad_maximum_fusion.2.halo), channel_id=1, source_target_pairs={{8,16},{16,8},{9,17},{17,9},{10,18},{18,10},{11,19},{19,11},{12,20... | collective-permute-start | bytes 98312 | tf_op jit(solution)/shard_map/ppermute | solution.py:45
  12.4 0.1 collective-permute-start.6
  12.5 0.7 %pad_maximum_fusion.1.gains = f32[11,1024]{1,0:T(8,128)S(1)} fusion(f32[9,1024]{1,0:T(8,128)S(1)} %reshape.18, f32[1,1024]{1,0:T(1,128)} %bitcast.9, f32[1,1024]{1,0:T(1,128)} %bitcast.10), kind=kLoop, calls=%fused_computation.2 | loop fusion | flops 22528 | bytes 90112 | tf_op jit(solution)/shard_map/concatenate | solution.py:380
  13.2 0.0 copy-start.5
  13.2 0.0 copy-start.6
  13.2 2.9 %copy.11 = bf16[1024,1024]{0,1:T(8,128)(2,1)S(1)} copy(bf16[1024,1024]{1,0:T(8,128)(2,1)} %param.16) | data formatting | bytes 4194304 | tf_op args[6]
  16.1 1.8 %collective-permute-done.4.halo_a = bf16[16,1024]{1,0:T(8,128)(2,1)S(1)} collective-permute-done((bf16[16,1024]{1,0:T(8,128)(2,1)S(1)}, bf16[16,1024]{1,0:T(8,128)(2,1)S(1)}, u32[]{:S(2)}, u32[]{:S(2)}) %collective-permute-start.4) | collective-permute-done | bytes 32800 | tf_op jit(solution)/shard_map/ppermute | solution.py:45
  17.9 3.3 %collective-permute-done.5.halo_b = bf16[16,1024]{1,0:T(8,128)(2,1)S(1)} collective-permute-done((bf16[16,1024]{1,0:T(8,128)(2,1)S(1)}, bf16[16,1024]{1,0:T(8,128)(2,1)S(1)}, u32[]{:S(2)}, u32[]{:S(2)}) %collective-permute-start.5) | collective-permute-done | bytes 32800 | tf_op jit(solution)/shard_map/ppermute | solution.py:45
  21.1 1.3 %collective-permute-done.6.ring_a = bf16[48,1024]{1,0:T(8,128)(2,1)S(1)} collective-permute-done((bf16[48,1024]{1,0:T(8,128)(2,1)S(1)}, bf16[48,1024]{1,0:T(8,128)(2,1)S(1)}, u32[]{:S(2)}, u32[]{:S(2)}) %collective-permute-start.6) | collective-permute-done | bytes 98336 | tf_op jit(solution)/shard_map/ppermute | solution.py:45
  22.4 0.0 collective-permute-done.tile_a
  22.4 0.0 collective-permute-done.1.tile_b
  22.5 3.3 %conv.1 = (bf16[128,1024]{1,0:T(8,128)(2,1)S(1)}, bf16[128,1024]{1,0:T(8,128)(2,1)}, bf16[128,1024]{1,0:T(8,128)(2,1)}, bf16[128,1024]{1,0:T(8,128)(2,1)S(1)}, bf16[128,1024]{1,0:T(8,128)(2,1)}) custom-call(bf16[8,16,1024]{2,1,0:T(8,128)(2,1)S(1)} %get-tuple-element.21.tok, bf16[8,16,1024]{2,1,0:T(8,128)(2,1)S(1)} %collective-permute-done.tile_a, ...), custom_call_target="tpu_custom_call" | custom-call | flops 16777216 | bytes 25165824 | tf_op jit(solution)/shard_map/conv/pallas_call | solution.py:401
  25.7 0.0 copy-start.3
  25.7 0.7 %copy-done.3 = bf16[128,1024]{1,0:T(8,128)(2,1)} copy-done((bf16[128,1024]{1,0:T(8,128)(2,1)}, bf16[128,1024]{1,0:T(8,128)(2,1)S(1)}, u32[]{:S(2)}) %copy-start.3) | copy-done | bytes 262168
  26.4 0.0 collective-permute-start.8
  26.4 0.5 collective-permute-start.10
  26.9 0.0 collective-permute-start.9
  26.9 0.7 %collective-permute-start.7 = (bf16[128,1024]{1,0:T(8,128)(2,1)}, bf16[128,1024]{1,0:T(8,128)(2,1)S(1)}, u32[]{:S(2)}, u32[]{:S(2)}) collective-permute-start(bf16[128,1024]{1,0:T(8,128)(2,1)} %get-tuple-element.25.refs_2_), channel_id=1, source_target_pairs={{1,2},{2,1},{3,4},{4,3},{5,6},{6,5},{7,0},{0,7},{9,10},{10,9},{11,... | collective-permute-start | bytes 786440 | tf_op jit(solution)/shard_map/ppermute | solution.py:45
  27.7 2.8 %collective-permute-start.11 = (bf16[128,1024]{1,0:T(8,128)(2,1)}, bf16[128,1024]{1,0:T(8,128)(2,1)S(1)}, u32[]{:S(2)}, u32[]{:S(2)}) collective-permute-start(bf16[128,1024]{1,0:T(8,128)(2,1)} %get-tuple-element.26.refs_3_), channel_id=1, source_target_pairs={{1,2},{2,1},{3,4},{4,3},{5,6},{6,5},{7,0},{0,7},{9,10},{10,9},{11,... | collective-permute-start | bytes 786440 | tf_op jit(solution)/shard_map/ppermute | solution.py:45
  30.5 0.0 collective-permute-done.8.refs_4_
  30.5 0.8 %collective-permute-start.12 = (bf16[128,1024]{1,0:T(8,128)(2,1)S(1)}, bf16[128,1024]{1,0:T(8,128)(2,1)S(1)}, u32[]{:S(2)}, u32[]{:S(2)}) collective-permute-start(bf16[128,1024]{1,0:T(8,128)(2,1)S(1)} %broadcast_select_fusion), channel_id=1, source_target_pairs={{1,2},{2,1},{3,4},{4,3},{5,6},{6,5},{7,0},{0,7},{9,10},{10,9},{11,... | collective-permute-start | bytes 786440 | tf_op jit(solution)/shard_map/ppermute | solution.py:45
  31.3 0.0 collective-permute-done.10.refs_6_
  31.3 0.0 collective-permute-done.9.refs_5_
  31.3 0.0 copy-done.5
  31.3 0.0 copy-done.6
  31.3 0.0 copy-start
  31.4 1.6 %copy-done = bf16[1024,1024]{1,0:T(8,128)(2,1)S(1)} copy-done((bf16[1024,1024]{1,0:T(8,128)(2,1)S(1)}, bf16[1024,1024]{1,0:T(8,128)(2,1)}, u32[]{:S(2)}) %copy-start) | copy-done | bytes 2097176
  32.9 0.0 copy-start.1
  32.9 1.6 %copy-done.1 = bf16[1024,1024]{1,0:T(8,128)(2,1)S(1)} copy-done((bf16[1024,1024]{1,0:T(8,128)(2,1)S(1)}, bf16[1024,1024]{1,0:T(8,128)(2,1)}, u32[]{:S(2)}) %copy-start.1) | copy-done | bytes 2097176
  34.5 0.0 copy-start.2
  34.5 7.0 %attend0_1_3_4_5.1 = (bf16[128,1024]{1,0:T(8,128)(2,1)S(1)}, f32[8,256]{1,0:T(8,128)S(1)}, f32[8,256]{1,0:T(8,128)S(1)}, f32[1024,128]{1,0:T(8,128)S(1)}) custom-call(s32[8]{0:T(128)S(1)} %bitcast.7, f32[16]{0:T(128)S(1)} %copy-done.6, bf16[128,1024]{1,0:T(8,128)(2,1)} %get-tuple-element.25.refs_2_, bf16[128,1024]{1,0:T(8,128)(2,1)} %get-tuple-element.26.refs_3_, ...), custom_call_target="tpu_custom_call" | custom-call | flops 68719476736 | bytes 268435456 | tf_op jit(solution)/shard_map/attend0_1_3_4_5/pallas_call | solution.py:336
  41.5 0.0 collective-permute-done.7.refs_2_
  41.6 0.1 collective-permute-start.13
  41.6 1.6 %collective-permute-done.11.refs_3_ = bf16[128,1024]{1,0:T(8,128)(2,1)S(1)} collective-permute-done((bf16[128,1024]{1,0:T(8,128)(2,1)}, bf16[128,1024]{1,0:T(8,128)(2,1)S(1)}, u32[]{:S(2)}, u32[]{:S(2)}) %collective-permute-start.11) | collective-permute-done | bytes 262176 | tf_op jit(solution)/shard_map/ppermute | solution.py:45
  43.2 4.5 %collective-permute-done.12.refs_4_ = bf16[128,1024]{1,0:T(8,128)(2,1)S(1)} collective-permute-done((bf16[128,1024]{1,0:T(8,128)(2,1)S(1)}, bf16[128,1024]{1,0:T(8,128)(2,1)S(1)}, u32[]{:S(2)}, u32[]{:S(2)}) %collective-permute-start.12) | collective-permute-done | bytes 262176 | tf_op jit(solution)/shard_map/ppermute | solution.py:45
  47.7 0.0 collective-permute-done.13.refs_5_
  47.7 0.0 copy-done.2
  47.7 0.0 copy-done.4
  47.7 6.0 %attend6_7_8_9.1 = bf16[128,1024]{1,0:T(8,128)(2,1)} custom-call(s32[8]{0:T(128)S(1)} %bitcast.8, f32[16]{0:T(128)S(1)} %copy-done.6, bf16[128,1024]{1,0:T(8,128)(2,1)S(1)} %collective-permute-done.7.refs_2_, bf16[128,1024]{1,0:T(8,128)(2,1)S(1)} %collective-permute-done.11.refs_3_, bf16[128,1024]{1,0:T(8,128)(2,1)S(1)} %collective-permute-done.12.refs_4_, ...), custom_call_target="tpu_custom_call" | custom-call | flops 68719476736 | bytes 268435456 | tf_op jit(solution)/shard_map/attend6_7_8_9/pallas_call | solution.py:336
  (6 shorter events, 0.1 us)
Async XLA Ops:
  1.0 8.8 %collective-permute-start.2 = (bf16[16,1024]{1,0:T(8,128)(2,1)S(1)}, bf16[16,1024]{1,0:T(8,128)(2,1)S(1)}, u32[]{:S(2)}, u32[]{:S(2)}) collective-permute-start(bf16[16,1024]{1,0:T(8,128)(2,1)S(1)} %get-tuple-element.22), channel_id=1, source_target_pairs={{1,2},{2,1},{3,4},{4,3},{5,6},{6,5},{7,0},{0,7},{9,10},{10,9},{11,... | collective-permute-start | bytes 98312 | tf_op jit(solution)/shard_map/ppermute | solution.py:45
  4.1 5.7 %collective-permute-start.3 = (bf16[16,1024]{1,0:T(8,128)(2,1)S(1)}, bf16[16,1024]{1,0:T(8,128)(2,1)S(1)}, u32[]{:S(2)}, u32[]{:S(2)}) collective-permute-start(bf16[16,1024]{1,0:T(8,128)(2,1)S(1)} %get-tuple-element.22), channel_id=1, source_target_pairs={{0,1},{1,0},{2,3},{3,2},{4,5},{5,4},{6,7},{7,6},{8,9},{9,8},{10,11... | collective-permute-start | bytes 98312 | tf_op jit(solution)/shard_map/ppermute | solution.py:45
  4.1 18.3 %collective-permute-start = (bf16[8,16,1024]{2,1,0:T(8,128)(2,1)}, bf16[8,16,1024]{2,1,0:T(8,128)(2,1)S(1)}, u32[]{:S(2)}, u32[]{:S(2)}) collective-permute-start(bf16[8,16,1024]{2,1,0:T(8,128)(2,1)} %tok.1), channel_id=1, source_target_pairs={{0,8},{8,0},{16,24},{24,16},{1,9},{9,1},{17,25},{25,17},{2,10},{10... | collective-permute-start | bytes 786440 | tf_op jit(solution)/shard_map/ppermute | solution.py:45
  4.7 17.8 %collective-permute-start.1 = (bf16[8,16,1024]{2,1,0:T(8,128)(2,1)}, bf16[8,16,1024]{2,1,0:T(8,128)(2,1)S(1)}, u32[]{:S(2)}, u32[]{:S(2)}) collective-permute-start(bf16[8,16,1024]{2,1,0:T(8,128)(2,1)} %tok.1), channel_id=1, source_target_pairs={{8,16},{16,8},{9,17},{17,9},{10,18},{18,10},{11,19},{19,11},{12,20... | collective-permute-start | bytes 786440 | tf_op jit(solution)/shard_map/ppermute | solution.py:45
  9.9 8.0 %collective-permute-start.4 = (bf16[16,1024]{1,0:T(8,128)(2,1)S(1)}, bf16[16,1024]{1,0:T(8,128)(2,1)S(1)}, u32[]{:S(2)}, u32[]{:S(2)}) collective-permute-start(bf16[16,1024]{1,0:T(8,128)(2,1)S(1)} %pad_maximum_fusion.2.halo), channel_id=1, source_target_pairs={{0,8},{8,0},{16,24},{24,16},{1,9},{9,1},{17,25},{25,17},{2,10},{10... | collective-permute-start | bytes 98312 | tf_op jit(solution)/shard_map/ppermute | solution.py:45
  10.0 11.1 %collective-permute-start.5 = (bf16[16,1024]{1,0:T(8,128)(2,1)S(1)}, bf16[16,1024]{1,0:T(8,128)(2,1)S(1)}, u32[]{:S(2)}, u32[]{:S(2)}) collective-permute-start(bf16[16,1024]{1,0:T(8,128)(2,1)S(1)} %pad_maximum_fusion.2.halo), channel_id=1, source_target_pairs={{8,16},{16,8},{9,17},{17,9},{10,18},{18,10},{11,19},{19,11},{12,20... | collective-permute-start | bytes 98312 | tf_op jit(solution)/shard_map/ppermute | solution.py:45
  12.4 10.0 %collective-permute-start.6 = (bf16[48,1024]{1,0:T(8,128)(2,1)S(1)}, bf16[48,1024]{1,0:T(8,128)(2,1)S(1)}, u32[]{:S(2)}, u32[]{:S(2)}) collective-permute-start(bf16[48,1024]{1,0:T(8,128)(2,1)S(1)} %pad_maximum_fusion), channel_id=1, source_target_pairs={{0,16},{16,0},{8,24},{24,8},{1,17},{17,1},{9,25},{25,9},{2,18},{18... | collective-permute-start | bytes 294920 | tf_op jit(solution)/shard_map/ppermute | solution.py:45
  13.2 18.1 %copy-start.5 = (s32[1,1,8]{2,1,0:T(1,128)S(1)}, s32[1,1,8]{2,1,0:T(1,128)}, u32[]{:S(2)}) copy-start(s32[1,1,8]{2,1,0:T(1,128)} %param.19) | copy-start | bytes 100
  13.2 18.1 %copy-start.6 = (f32[16]{0:T(128)S(1)}, f32[16]{0:T(128)}, u32[]{:S(2)}) copy-start(f32[16]{0:T(128)} %refs_1_.3) | copy-start | bytes 196
  25.7 0.7 %copy-start.3 = (bf16[128,1024]{1,0:T(8,128)(2,1)}, bf16[128,1024]{1,0:T(8,128)(2,1)S(1)}, u32[]{:S(2)}) copy-start(bf16[128,1024]{1,0:T(8,128)(2,1)S(1)} %get-tuple-element.36.refs_14_) | copy-start | bytes 786436
  26.4 4.1 %collective-permute-start.8 = (bf16[128,1024]{1,0:T(8,128)(2,1)}, bf16[128,1024]{1,0:T(8,128)(2,1)S(1)}, u32[]{:S(2)}, u32[]{:S(2)}) collective-permute-start(bf16[128,1024]{1,0:T(8,128)(2,1)} %get-tuple-element.25.refs_2_), channel_id=1, source_target_pairs={{0,1},{1,0},{2,3},{3,2},{4,5},{5,4},{6,7},{7,6},{8,9},{9,8},{10,11... | collective-permute-start | bytes 786440 | tf_op jit(solution)/shard_map/ppermute | solution.py:45
  26.4 4.9 %collective-permute-start.10 = (bf16[128,1024]{1,0:T(8,128)(2,1)}, bf16[128,1024]{1,0:T(8,128)(2,1)S(1)}, u32[]{:S(2)}, u32[]{:S(2)}) collective-permute-start(bf16[128,1024]{1,0:T(8,128)(2,1)} %get-tuple-element.27), channel_id=1, source_target_pairs={{0,1},{1,0},{2,3},{3,2},{4,5},{5,4},{6,7},{7,6},{8,9},{9,8},{10,11... | collective-permute-start | bytes 786440 | tf_op jit(solution)/shard_map/ppermute | solution.py:45
  26.9 4.4 %collective-permute-start.9 = (bf16[128,1024]{1,0:T(8,128)(2,1)}, bf16[128,1024]{1,0:T(8,128)(2,1)S(1)}, u32[]{:S(2)}, u32[]{:S(2)}) collective-permute-start(bf16[128,1024]{1,0:T(8,128)(2,1)} %get-tuple-element.26.refs_3_), channel_id=1, source_target_pairs={{0,1},{1,0},{2,3},{3,2},{4,5},{5,4},{6,7},{7,6},{8,9},{9,8},{10,11... | collective-permute-start | bytes 786440 | tf_op jit(solution)/shard_map/ppermute | solution.py:45
  26.9 14.6 %collective-permute-start.7 = (bf16[128,1024]{1,0:T(8,128)(2,1)}, bf16[128,1024]{1,0:T(8,128)(2,1)S(1)}, u32[]{:S(2)}, u32[]{:S(2)}) collective-permute-start(bf16[128,1024]{1,0:T(8,128)(2,1)} %get-tuple-element.25.refs_2_), channel_id=1, source_target_pairs={{1,2},{2,1},{3,4},{4,3},{5,6},{6,5},{7,0},{0,7},{9,10},{10,9},{11,... | collective-permute-start | bytes 786440 | tf_op jit(solution)/shard_map/ppermute | solution.py:45
  27.7 15.5 %collective-permute-start.11 = (bf16[128,1024]{1,0:T(8,128)(2,1)}, bf16[128,1024]{1,0:T(8,128)(2,1)S(1)}, u32[]{:S(2)}, u32[]{:S(2)}) collective-permute-start(bf16[128,1024]{1,0:T(8,128)(2,1)} %get-tuple-element.26.refs_3_), channel_id=1, source_target_pairs={{1,2},{2,1},{3,4},{4,3},{5,6},{6,5},{7,0},{0,7},{9,10},{10,9},{11,... | collective-permute-start | bytes 786440 | tf_op jit(solution)/shard_map/ppermute | solution.py:45
  30.5 17.2 %collective-permute-start.12 = (bf16[128,1024]{1,0:T(8,128)(2,1)S(1)}, bf16[128,1024]{1,0:T(8,128)(2,1)S(1)}, u32[]{:S(2)}, u32[]{:S(2)}) collective-permute-start(bf16[128,1024]{1,0:T(8,128)(2,1)S(1)} %broadcast_select_fusion), channel_id=1, source_target_pairs={{1,2},{2,1},{3,4},{4,3},{5,6},{6,5},{7,0},{0,7},{9,10},{10,9},{11,... | collective-permute-start | bytes 786440 | tf_op jit(solution)/shard_map/ppermute | solution.py:45
  31.3 1.6 %copy-start = (bf16[1024,1024]{1,0:T(8,128)(2,1)S(1)}, bf16[1024,1024]{1,0:T(8,128)(2,1)}, u32[]{:S(2)}) copy-start(bf16[1024,1024]{1,0:T(8,128)(2,1)} %refs_9_.1) | copy-start | bytes 6291460
  32.9 1.6 %copy-start.1 = (bf16[1024,1024]{1,0:T(8,128)(2,1)S(1)}, bf16[1024,1024]{1,0:T(8,128)(2,1)}, u32[]{:S(2)}) copy-start(bf16[1024,1024]{1,0:T(8,128)(2,1)} %refs_7_.3) | copy-start | bytes 6291460
  34.5 13.2 %copy-start.2 = (bf16[1024,1024]{1,0:T(8,128)(2,1)S(1)}, bf16[1024,1024]{1,0:T(8,128)(2,1)}, u32[]{:S(2)}) copy-start(bf16[1024,1024]{1,0:T(8,128)(2,1)} %refs_13_.1) | copy-start | bytes 6291460
  34.5 13.2 %copy-start.4 = (bf16[128,1024]{1,0:T(8,128)(2,1)S(1)}, bf16[128,1024]{1,0:T(8,128)(2,1)}, u32[]{:S(2)}) copy-start(bf16[128,1024]{1,0:T(8,128)(2,1)} %copy-done.3) | copy-start | bytes 786436
  41.6 6.2 %collective-permute-start.13 = (bf16[128,1024]{1,0:T(8,128)(2,1)S(1)}, bf16[128,1024]{1,0:T(8,128)(2,1)S(1)}, u32[]{:S(2)}, u32[]{:S(2)}) collective-permute-start(bf16[128,1024]{1,0:T(8,128)(2,1)S(1)} %collective-permute-done.7.refs_2_), channel_id=1, source_target_pairs={{0,1},{1,0},{2,3},{3,2},{4,5},{5,4},{6,7},{7,6},{8,9},{9,8},{10,11... | collective-permute-start | bytes 786440 | tf_op jit(solution)/shard_map/ppermute | solution.py:45
